TPU v7x, 32 devices: a whole 2x2x4 slice. The times are simulated.
32 devices in a mesh: sec: 2 (over core), grp: 4 (over y, x), dev: 4 (over z).
Axes of the slice: x: 2, y: 2, z: 4, core: 2. Of those that a mesh axis runs over, the one named last changes fastest.
Arguments:
- current: float32 [32, 196608], P(None, ('sec', 'grp', 'dev')), may hold values from -6 to 6
- prior: float32 [8, 32, 196608], P(None, None, ('sec', 'grp', 'dev')), as said below
- block_values: float32 [1024, 6, 9216], P(('grp', 'dev')), may hold values from -0.25 to 0.25
- block_cols: int32 [1024, 6], P(('grp', 'dev')), may hold values from 0 to 63
- face_match: int32 [16, 4, 1536], P(('grp', 'dev')), may hold values from 0 to 1535, each once within a row
- face_weight: float32 [16, 4, 1536], P(('grp', 'dev')), may hold values from -3 to 3
- fluid_diag: float32 [98304], P(('grp', 'dev')), may hold values from 2 to 4
- wet_source: int32 [49152], P(('grp', 'dev')), may hold values from 0 to 6143
- wet_dest: int32 [49152, 1], P(('grp', 'dev')), may hold values from 0 to 15; in each aligned block of 3072 rows (0 to 3071, 3072 to 6143, ...) at most 392 rows name the same one
- wet_target: int32 [49152], P(('grp', 'dev')), may hold values from 0 to 6143
- wet_weight: float32 [49152], P(('grp', 'dev')), may hold values from -5 to 5
Outputs:
- next_block: float32 [32, 196608], P(None, ('sec', 'grp', 'dev'))
- coeffs: float32 [8, 32, 32], replicated
- rfac: float32 [32, 32], replicated
Inputs may be any that keep to these rules, and one draw needn't show every extreme that they name: `block_cols`: block columns index blocks within the same subdomain. `face_match`: each subdomain's matching of one round is a permutation of its face. `prior`: each earlier block's columns have about unit length. `wet_dest`: among one structure subdomain's couplings, at most 392 name the same fluid subdomain, and some subdomain has exactly 392 for one.
All inputs are finite; a program needn't handle non-finite values.
Results may differ from a plain program's by a relative error of at most 0.00008.
Values sent between devices are 32-bit elements; how exact they have to be, the bound alone decides.
A program may use at most 128 MiB of HBM per device.

v0:
```python
import jax
import jax.numpy as jnp
from jax import lax
from jax.sharding import PartitionSpec as P

BS = 96
NB = 6
ROUNDS = 4


def swapped(block, axis, bit):
    count = lax.axis_size(axis)
    route = []
    for low in range(count):
        high = low | 1 << bit
        if high != low and high < count:
            route += [(low, high), (high, low)]
    return lax.ppermute(block, axis, route)


def with_halo(x, sides, width):
    for axis, dim in sides:
        count, length = (lax.axis_size(axis), x.shape[dim])
        up = [(i, (i + 1) % count) for i in range(count - 1)]
        down = [(j, i) for i, j in up]
        last = lax.slice_in_dim(x, length - width, length, axis=dim)
        initial = lax.slice_in_dim(x, 0, width, axis=dim)
        before = lax.ppermute(last, axis, up)
        after = lax.ppermute(initial, axis, down)
        x = jnp.concatenate([before, x, after], axis=dim)
    return x


def shards(
    current,
    prior,
    block_values,
    block_cols,
    face_match,
    face_weight,
    fluid_diag,
    wet_source,
    wet_dest,
    wet_target,
    wet_weight,
):
    highest = lax.Precision.HIGHEST
    width = current.shape[0]
    local_rows = current.shape[1]
    face_rows = face_match.shape[2]
    row_blocks = block_cols.shape[0]
    wet_slots = wet_source.shape[0]
    subdomains = lax.axis_size("grp") * lax.axis_size("dev")
    total_rows = local_rows * lax.axis_size("sec") * subdomains
    capacity = 2 * wet_slots // subdomains + 8
    is_shell = lax.axis_index("sec") == 0
    senders = jnp.where(is_shell, 1.0, 0.0).astype(jnp.float32)
    partner_faces = []
    for sweep in range(ROUNDS):
        face_now = current[:, sweep * face_rows : (sweep + 1) * face_rows]
        if sweep < 2:
            partner_faces.append(swapped(face_now, "dev", sweep))
        else:
            partner_faces.append(swapped(face_now, "grp", sweep - 2))
    padded = with_halo(current, ((("grp", "dev"), 1),), 1)
    destination = wet_dest[:, 0]
    onehot = (destination[:, None] == jnp.arange(subdomains, dtype=jnp.int32)[None, :]).astype(
        jnp.int32
    )
    ranks = jnp.cumsum(onehot, axis=0) - 1
    slot = jnp.sum(ranks * onehot, axis=1)
    moved = (wet_weight * senders)[None, :] * current[:, wet_source]
    target_float = wet_target.astype(jnp.float32) * senders
    buffer = jnp.zeros((2 * subdomains, width, capacity), jnp.float32)
    buffer = buffer.at[destination + subdomains, :, slot].set(moved.T)
    row_buffer = jnp.zeros((2 * subdomains, capacity), jnp.float32)
    row_buffer = row_buffer.at[destination + subdomains, slot].set(target_float)
    got_values, got_rows = (
        lax.all_to_all(buffer, ("sec", "grp", "dev"), split_axis=0, concat_axis=0, tiled=True),
        lax.all_to_all(row_buffer, ("sec", "grp", "dev"), split_axis=0, concat_axis=0, tiled=True),
    )
    incoming = jnp.moveaxis(got_values, 1, 0).reshape(width, -1)
    incoming_rows = got_rows.reshape(-1).astype(jnp.int32)

    def shell_apply(vector):
        picked = vector.reshape(width, row_blocks, BS)[:, block_cols, :]
        matrices = block_values.reshape(row_blocks, NB, BS, BS)
        result = jnp.einsum("kibc,ibrc->kir", picked, matrices, precision=highest).reshape(
            width, local_rows
        )
        for sweep in range(ROUNDS):
            matched = partner_faces[sweep][:, face_match[0, sweep]]
            result = result.at[:, sweep * face_rows : (sweep + 1) * face_rows].add(
                face_weight[0, sweep][None, :] * matched
            )
        return result

    def fluid_apply(vector):
        before = padded[:, :-2]
        after = padded[:, 2:]
        result = fluid_diag[None, :] * vector - before - after
        return result.at[:, incoming_rows].add(incoming)

    image = lax.cond(is_shell, shell_apply, fluid_apply, current)
    h_first = lax.psum(
        jnp.einsum("jkr,lr->jkl", prior, image, precision=highest), ("sec", "grp", "dev")
    )
    w_one = image - jnp.einsum("jkl,jkr->lr", h_first, prior, precision=highest)
    h_second = lax.psum(
        jnp.einsum("jkr,lr->jkl", prior, w_one, precision=highest), ("sec", "grp", "dev")
    )
    w_two = w_one - jnp.einsum("jkl,jkr->lr", h_second, prior, precision=highest)
    gram = lax.psum(jnp.dot(w_two, w_two.T, precision=highest), ("sec", "grp", "dev")) / total_rows
    coeffs = h_first + h_second
    factor = jnp.linalg.cholesky(gram)
    next_block = lax.linalg.triangular_solve(factor, w_two, left_side=True, lower=True)
    return (next_block, coeffs, factor.T)


def solution(mesh):
    placed = (
        P(None, ("sec", "grp", "dev")),
        P(None, None, ("sec", "grp", "dev")),
        P(("grp", "dev"), None, None),
        P(("grp", "dev"), None),
        P(("grp", "dev"), None, None),
        P(("grp", "dev"), None, None),
        P(("grp", "dev")),
        P(("grp", "dev")),
        P(("grp", "dev"), None),
        P(("grp", "dev")),
        P(("grp", "dev")),
    )
    return jax.shard_map(
        shards,
        mesh=mesh,
        in_specs=placed,
        out_specs=(P(None, ("sec", "grp", "dev")), P(), P()),
        check_vma=False,
    )
```

profile of v0, /device:TPU:0, one launch (start us, length us, event | category | flops | bytes accessed | tf_op | source)
XLA Modules:
  0.0 428.3 jit_solution(6008046726579395630)
XLA Ops:
  1.4 4.6 %reduce-window.6 = s32[16,24,128]{2,1,0:T(8,128)S(1)} reduce-window(s32[16,24,128]{2,1,0:T(8,128)S(1)} %fusion.27, s32[]{:T(128)} %constant.179.clone.1), window={size=1x1x128 pad=0_0x0_0x127_0}, to_apply=%region_0.1 | reduce-window | flops 6242304 | bytes 393220 | tf_op jit(solution)/shard_map/reduce-window
  6.7 0.8 fusion.26
  8.2 0.8 and_reduce_fusion
  10.5 11.8 %scatter_custom_fusion.1 = f32[12544]{0:T(1024)S(1)} fusion(s32[3072]{0:T(1024)S(1)} %broadcast_select_fusion, f32[3072]{0:T(1024)S(1)} %get-tuple-element.233, f32[]{:T(128)} %constant.180.clone.1), kind=kCustom, calls=%fused_computation.71 | custom fusion | bytes 50180
  22.3 0.8 all_to_all.9
  23.1 7.3 %all-to-all-start = ((f32[32,1,392]{2,1,0:T(1,128)}), f32[32,1,392]{2,1,0:T(1,128)S(1)}, u32[]{:S(2)}, u32[]{:S(2)}) async-start(f32[32,1,392]{2,1,0:T(1,128)} %all_to_all.9), calls=%async_computation | async-start | bytes 131072 | tf_op jit(solution)/shard_map/all_to_all | solution.py:80
  31.2 2.0 copy.123
  33.1 20.8 %scatter_custom_fusion.2 = f32[12544,32]{1,0:T(8,128)} fusion(s32[3072]{0:T(1024)S(1)} %broadcast_select_fusion, f32[]{:T(128)} %constant.180.clone.1, f32[3072]{0:T(1024)S(1)} %get-tuple-element.234, f32[32,6144]{0,1:T(8,128)S(1)} %copy.123, s32[3072]{0:T(1024)S(1)} %fusion.34), kind=kCustom, calls=%fused_computation.50 | custom fusion | flops 98304 | bytes 4775940
  53.9 6.0 %copy.125 = f32[32,32,392]{2,1,0:T(8,128)} copy(f32[32,32,392]{1,2,0:T(8,128)} %bitcast.92) | data formatting | bytes 3211264 | tf_op jit(solution)/shard_map/scatter | solution.py:75
  60.0 5.8 %all-to-all-start.1 = ((f32[32,32,392]{2,1,0:T(8,128)}), f32[32,32,392]{2,1,0:T(8,128)S(1)}, u32[]{:S(2)}, u32[]{:S(2)}) async-start(f32[32,32,392]{2,1,0:T(8,128)} %copy.125), calls=%async_computation.1 | async-start | bytes 4194304 | tf_op jit(solution)/shard_map/all_to_all | solution.py:79
  65.9 0.8 fusion.36
  66.7 1.8 collective-permute-start.2
  68.4 2.4 collective-permute-start.3
  70.8 1.5 collective-permute-start.4
  72.3 1.5 collective-permute-start.5
  73.9 2.4 collective-permute-start
  76.3 33.0 %collective-permute-done = f32[32,1]{1,0:T(8,128)S(1)} collective-permute-done((f32[32,1]{1,0:T(8,128)S(1)}, f32[32,1]{1,0:T(8,128)S(1)}, u32[]{:S(2)}, u32[]{:S(2)}) %collective-permute-start) | collective-permute-done | bytes 160 | tf_op jit(solution)/shard_map/ppermute | solution.py:28
  109.3 1.3 collective-permute-start.1
  110.6 15.2 %collective-permute-done.1 = f32[32,1]{1,0:T(8,128)S(1)} collective-permute-done((f32[32,1]{1,0:T(8,128)S(1)}, f32[32,1]{1,0:T(8,128)S(1)}, u32[]{:S(2)}, u32[]{:S(2)}) %collective-permute-start.1) | collective-permute-done | bytes 160 | tf_op jit(solution)/shard_map/ppermute | solution.py:29
  125.8 1.2 concatenate.15
  127.1 81.3 %conditional.1 = (f32[32,6144]{0,1:T(8,128)}) conditional(s32[]{:T(128)} %convert_element_type.23, (f32[6144]{0:T(1024)S(1)}, f32[32,6144]{1,0:T(8,128)S(1)}, f32[32,6146]{1,0:T(8,128)}, f32[32,1,392]{2,1,0:T(1,128)S(1)}, f32[32,32,392]{2,0,1:T(8,128)S(1)}) %tuple.73, (f32[32,6144]{1,0:T(8,128)S(1)}, s32[64,6]{0,1:T(8,128)S(1)}, ...), branch_computations={%region_5.7_spmd, %region_7.11_spmd} | conditional | flops 1359523968 | bytes 72574472 | solution.py:104
  135.4 3.8 gather_fusion
  139.2 17.6 %reshape.288 = f32[64,6,96,96]{3,2,0,1:T(8,128)} reshape(f32[64,6,9216]{2,0,1:T(8,128)} %get-tuple-element.106) | data formatting | bytes 28311552 | tf_op jit(solution)/shard_map/cond/branch_1_fun/reshape | solution.py:87
  156.8 20.7 %fusion.2 = f32[32,64,96]{2,0,1:T(8,128)S(1)} fusion(f32[32,64,6,96]{3,0,2,1:T(8,128)} %bitcast.91, f32[64,6,96,96]{3,2,0,1:T(8,128)} %reshape.288), kind=kOutput, calls=%fused_computation.11 | convolution fusion | flops 1358954496 | bytes 19660800 | tf_op jit(solution)/shard_map/cond/branch_1_fun/kibc,ibrc->kir/dot_general | solution.py:88
  177.5 2.3 copy.146
  179.8 1.2 copy.130
  181.1 2.6 gather_fusion.1
  184.4 2.9 fusion.5
  187.3 1.2 copy.131
  188.5 2.6 gather_fusion.2
  191.8 2.9 fusion.6
  194.7 1.2 copy.132
  195.9 2.6 gather_fusion.3
  199.2 3.0 fusion.7
  202.2 1.2 copy.133
  203.4 2.6 gather_fusion.4
  206.0 2.4 fusion.8
  208.3 2.3 copy.135
  210.7 22.2 %fusion.20 = f32[8,32,32]{1,2,0:T(8,128)S(1)} fusion(f32[8,32,6144]{2,1,0:T(8,128)} %param.22, f32[32,6144]{0,1:T(8,128)} %get-tuple-element.235), kind=kOutput, calls=%fused_computation.56 | convolution fusion | flops 603979776 | bytes 7110656 | tf_op jit(solution)/shard_map/jkr,lr->jkl/dot_general | solution.py:106
  232.8 71.6 %psum.21 = f32[8,32,32]{1,2,0:T(8,128)S(1)} all-reduce(f32[8,32,32]{1,2,0:T(8,128)S(1)} %fusion.20), channel_id=1, replica_groups=mesh['sec'=2,'grp'=4,'dev'=4] {'sec','grp','dev'}, use_global_device_ids=true, to_apply=%region_11.12 | all-reduce | flops 8192 | bytes 65536 | tf_op jit(solution)/shard_map/psum | solution.py:105
  304.5 7.5 %convolution_bitcast_fusion.1 = f32[32,6144]{1,0:T(8,128)S(1)} fusion(f32[8,32,32]{1,2,0:T(8,128)S(1)} %psum.21, f32[8,32,6144]{2,1,0:T(8,128)} %param.22), kind=kOutput, calls=%fused_computation.48 | convolution fusion | flops 603979776 | bytes 7110656 | tf_op jit(solution)/shard_map/jkl,jkr->lr/dot_general | solution.py:108
  312.1 16.3 %convolution_bitcast_fusion.2 = f32[8,32,32]{1,2,0:T(8,128)S(1)} fusion(f32[8,32,6144]{2,1,0:T(8,128)} %param.22, f32[32,6144]{1,0:T(8,128)S(1)} %sub.23), kind=kOutput, calls=%fused_computation.55 | convolution fusion | flops 603979776 | bytes 7110656 | tf_op jit(solution)/shard_map/jkr,lr->jkl/dot_general | solution.py:110
  328.4 39.9 %psum.22 = f32[8,32,32]{1,2,0:T(8,128)S(1)} all-reduce(f32[8,32,32]{1,2,0:T(8,128)S(1)} %convolution_bitcast_fusion.2), channel_id=1, replica_groups=mesh['sec'=2,'grp'=4,'dev'=4] {'sec','grp','dev'}, use_global_device_ids=true, to_apply=%region_12.13 | all-reduce | flops 8192 | bytes 65536 | tf_op jit(solution)/shard_map/psum | solution.py:109
  368.3 7.6 %fusion.14 = f32[32,6144]{1,0:T(8,128)S(1)} fusion(f32[32,6144]{1,0:T(8,128)S(1)} %sub.23, f32[8,32,32]{1,2,0:T(8,128)S(1)} %psum.22, f32[8,32,6144]{2,1,0:T(8,128)} %param.22), kind=kOutput, calls=%fused_computation.49 | convolution fusion | flops 604176384 | bytes 7897088 | tf_op jit(solution)/shard_map/jkl,jkr->lr/dot_general | solution.py:112
  376.7 41.2 %psum.23 = f32[32,32]{0,1:T(8,128)S(1)} all-reduce(f32[32,32]{0,1:T(8,128)S(1)} %fusion.38), channel_id=1, replica_groups=mesh['sec'=2,'grp'=4,'dev'=4] {'sec','grp','dev'}, use_global_device_ids=true, to_apply=%region_13.14 | all-reduce | flops 1024 | bytes 8192 | tf_op jit(solution)/shard_map/psum | solution.py:113
  418.0 2.9 cholesky.16
  422.2 2.4 custom-call.6
  424.7 1.7 fusion.30
  (50 shorter events, 11.6 us)
Async XLA Ops:
  23.1 36.9 %all-to-all-start = ((f32[32,1,392]{2,1,0:T(1,128)}), f32[32,1,392]{2,1,0:T(1,128)S(1)}, u32[]{:S(2)}, u32[]{:S(2)}) async-start(f32[32,1,392]{2,1,0:T(1,128)} %all_to_all.9), calls=%async_computation | async-start | bytes 131072 | tf_op jit(solution)/shard_map/all_to_all | solution.py:80
  60.0 5.9 %copy-start = (f32[32,6144]{1,0:T(8,128)S(1)}, f32[32,6144]{1,0:T(8,128)}, u32[]{:S(2)}) copy-start(f32[32,6144]{1,0:T(8,128)} %param.21) | copy-start | bytes 2359300
  60.0 67.0 %copy-start.3 = (f32[1,4,1536]{2,1,0:T(4,128)S(1)}, f32[1,4,1536]{2,1,0:T(4,128)}, u32[]{:S(2)}) copy-start(f32[1,4,1536]{2,1,0:T(4,128)} %param.26) | copy-start | bytes 73732
  60.0 67.0 %copy-start.4 = (s32[1,4,1536]{2,1,0:T(4,128)S(1)}, s32[1,4,1536]{2,1,0:T(4,128)}, u32[]{:S(2)}) copy-start(s32[1,4,1536]{2,1,0:T(4,128)} %param.25) | copy-start | bytes 73732
  60.0 67.1 %copy-start.5 = (f32[6144]{0:T(1024)S(1)}, f32[6144]{0:T(1024)}, u32[]{:S(2)}) copy-start(f32[6144]{0:T(1024)} %param.27) | copy-start | bytes 73732
  60.0 67.1 %copy-start.6 = (s32[64,6]{0,1:T(8,128)S(1)}, s32[64,6]{0,1:T(8,128)}, u32[]{:S(2)}) copy-start(s32[64,6]{0,1:T(8,128)} %param.24) | copy-start | bytes 4612
  60.0 67.0 %all-to-all-start.1 = ((f32[32,32,392]{2,1,0:T(8,128)}), f32[32,32,392]{2,1,0:T(8,128)S(1)}, u32[]{:S(2)}, u32[]{:S(2)}) async-start(f32[32,32,392]{2,1,0:T(8,128)} %copy.125), calls=%async_computation.1 | async-start | bytes 4194304 | tf_op jit(solution)/shard_map/all_to_all | solution.py:79
  66.7 60.3 %collective-permute-start.2 = (f32[32,1536]{1,0:T(8,128)}, f32[32,1536]{1,0:T(8,128)}, u32[]{:S(2)}, u32[]{:S(2)}) collective-permute-start(f32[32,1536]{1,0:T(8,128)} %get-tuple-element.226), channel_id=1, source_target_pairs={{0,1},{1,0},{2,3},{3,2},{4,5},{5,4},{6,7},{7,6},{8,9},{9,8},{10,11... | collective-permute-start | bytes 589832 | tf_op jit(solution)/shard_map/ppermute | solution.py:18
  68.4 58.6 %collective-permute-start.3 = (f32[32,1536]{1,0:T(8,128)}, f32[32,1536]{1,0:T(8,128)}, u32[]{:S(2)}, u32[]{:S(2)}) collective-permute-start(f32[32,1536]{1,0:T(8,128)} %get-tuple-element.225), channel_id=1, source_target_pairs={{0,2},{2,0},{1,3},{3,1},{4,6},{6,4},{5,7},{7,5},{8,10},{10,8},{9,1... | collective-permute-start | bytes 589832 | tf_op jit(solution)/shard_map/ppermute | solution.py:18
  70.8 56.1 %collective-permute-start.4 = (f32[32,1536]{1,0:T(8,128)S(1)}, f32[32,1536]{1,0:T(8,128)}, u32[]{:S(2)}, u32[]{:S(2)}) collective-permute-start(f32[32,1536]{1,0:T(8,128)S(1)} %get-tuple-element.224), channel_id=1, source_target_pairs={{0,4},{4,0},{8,12},{12,8},{1,5},{5,1},{9,13},{13,9},{2,6},{6,2},{1... | collective-permute-start | bytes 589832 | tf_op jit(solution)/shard_map/ppermute | solution.py:18
  72.3 54.7 %collective-permute-start.5 = (f32[32,1536]{1,0:T(8,128)S(1)}, f32[32,1536]{1,0:T(8,128)}, u32[]{:S(2)}, u32[]{:S(2)}) collective-permute-start(f32[32,1536]{1,0:T(8,128)S(1)} %get-tuple-element.223), channel_id=1, source_target_pairs={{0,8},{8,0},{4,12},{12,4},{1,9},{9,1},{5,13},{13,5},{2,10},{10,2},... | collective-permute-start | bytes 589832 | tf_op jit(solution)/shard_map/ppermute | solution.py:18
  73.9 35.4 %collective-permute-start = (f32[32,1]{1,0:T(8,128)S(1)}, f32[32,1]{1,0:T(8,128)S(1)}, u32[]{:S(2)}, u32[]{:S(2)}) collective-permute-start(f32[32,1]{1,0:T(8,128)S(1)} %get-tuple-element.228), channel_id=1, source_target_pairs={{0,1},{1,2},{2,3},{3,4},{4,5},{5,6},{6,7},{7,8},{8,9},{9,10},{10,1... | collective-permute-start | bytes 392 | tf_op jit(solution)/shard_map/ppermute | solution.py:28
  109.3 16.5 %collective-permute-start.1 = (f32[32,1]{1,0:T(8,128)S(1)}, f32[32,1]{1,0:T(8,128)S(1)}, u32[]{:S(2)}, u32[]{:S(2)}) collective-permute-start(f32[32,1]{1,0:T(8,128)S(1)} %get-tuple-element.227), channel_id=1, source_target_pairs={{1,0},{2,1},{3,2},{4,3},{5,4},{6,5},{7,6},{8,7},{9,8},{10,9},{11,1... | collective-permute-start | bytes 392 | tf_op jit(solution)/shard_map/ppermute | solution.py:29
where the time goes:
time: 435 us; the launch traced here: 428 us
  blocking collectives  153 us (35%)
  matrix products  76.7 us (18%)
  local copies, waits for them, and re-layouts  67.1 us (15%)
  other arithmetic  51 us (12%)
  waiting for transfers between devices  48.2 us (11%)
  starting transfers between devices  24 us (6%)
  loops' own time  7.2 us (2%)
    psum x1, blocking collectives, shards(): lax.psum(jnp.einsum('jkr,lr->jkl', prior, image, precision=highest), ('se...  71.6 us
    psum x1, blocking collectives, shards(): lax.psum(jnp.dot(w_two, w_two.T, precision=highest), ('sec', 'grp', 'dev'))  41.2 us
    psum x1, blocking collectives, shards(): lax.psum(jnp.einsum('jkr,lr->jkl', prior, w_one, precision=highest), ('se...  39.9 us
    ppermute x1, waiting for transfers between devices, with_halo(): before = lax.ppermute(last, axis, up)  33 us
    unnamed x4, other arithmetic  22.4 us
    dot_general x1, matrix products, shards(): jnp.einsum('jkr,lr->jkl', prior, image, precision=highest)  22.2 us
    dot_general x1, matrix products, shell_apply(): jnp.einsum('kibc,ibrc->kir', picked, matrices, precision=highest)  20.7 us
    reshape x1, local copies, waits for them, and re-layouts, shell_apply(): matrices = block_values.reshape(row_blocks, NB, BS, BS)  17.6 us
  transfers between devices with their start and end apart: 8, of which 2 were waited for; matrix products, arithmetic and copies ran while one was open for 7% of the time, Pallas kernels for 0%

commit v1 on v0

v1 whole, which is shorter than its diff:
```python
import functools

import jax
import jax.numpy as jnp
from jax import lax
from jax.experimental import pallas as pl
from jax.experimental.pallas import tpu as pltpu
from jax.sharding import PartitionSpec as P

BS = 96
NB = 6
ROUNDS = 4
LANES = 128
META = 8
F32 = jnp.float32
BF16 = jnp.bfloat16
NT = (((1,), (1,)), ((), ()))
ALL = ("sec", "grp", "dev")


def split2(x):
    hi = x.astype(BF16)
    return hi, (x - hi.astype(F32)).astype(BF16)


def nt(a, b):
    return lax.dot_general(a, b, NT, preferred_element_type=F32)


def lane_gather(x, low):
    return jnp.take_along_axis(x, low, axis=1)


def pack_kernel(subdomains, per, x_ref, src_ref, dest_ref, tgt_ref, w_ref, out_ref, meta_ref):
    width, rows = x_ref.shape
    blocks = src_ref.shape[0]
    slabs = subdomains * per
    dest = dest_ref[...]
    lane = lax.broadcasted_iota(jnp.int32, (LANES, LANES), 1)
    sub = lax.broadcasted_iota(jnp.int32, (LANES, LANES), 0)
    tri = jnp.where(sub < lane, 1.0, 0.0).astype(BF16)
    ones = jnp.ones((LANES, LANES), BF16)
    low_tri = jnp.where(
        lax.broadcasted_iota(jnp.int32, (blocks, blocks), 1)
        < lax.broadcasted_iota(jnp.int32, (blocks, blocks), 0),
        1.0,
        0.0,
    ).astype(BF16)

    def count(q, rank):
        mine = dest == q
        oh = jnp.where(mine, 1.0, 0.0).astype(BF16)
        within = jnp.dot(oh, tri, preferred_element_type=F32)
        totals = jnp.dot(oh, ones, preferred_element_type=F32).astype(BF16)
        offset = jnp.dot(low_tri, totals, preferred_element_type=F32)
        return jnp.where(mine, within + offset, rank)

    rank = lax.fori_loop(0, subdomains, count, jnp.zeros(dest.shape, F32)).astype(jnp.int32)
    slab = dest * per + rank // LANES
    spot = rank % LANES
    src = src_ref[...]
    tgt = tgt_ref[...]
    w = w_ref[...]
    w0 = w.astype(BF16).astype(F32)
    w1 = (w - w0).astype(BF16).astype(F32)
    w2 = w - w0 - w1
    fields = [src // LANES, src % LANES, tgt // LANES, tgt % LANES]
    fields = [f.astype(F32) for f in fields] + [w0, w1, w2]
    acc = jnp.zeros((len(fields) * slabs, LANES), F32)
    slab_row = lax.broadcasted_iota(jnp.int32, (slabs, LANES), 0)
    for i in range(blocks):
        hit = slab_row == slab[i : i + 1, :]
        lhs = jnp.concatenate([jnp.where(hit, f[i : i + 1, :], 0.0) for f in fields], axis=0)
        oh = jnp.where(sub == spot[i : i + 1, :], 1.0, 0.0)
        acc = acc + nt(lhs.astype(BF16), oh.astype(BF16))
    parts = [acc[f * slabs : (f + 1) * slabs] for f in range(len(fields))]
    meta_ref[0] = parts[0]
    meta_ref[1] = parts[1]
    meta_ref[2] = parts[2] * LANES + parts[3]
    meta_ref[3] = parts[4] + parts[5] + parts[6]

    def gather(a, carry):
        row = pl.ds(a, 1)
        high = jnp.broadcast_to(meta_ref[0, row, :].astype(jnp.int32), (width, LANES))
        low = jnp.broadcast_to(meta_ref[1, row, :].astype(jnp.int32), (width, LANES))
        got = jnp.zeros((width, LANES), F32)
        for h in range(rows // LANES):
            piece = lane_gather(x_ref[:, h * LANES : (h + 1) * LANES], low)
            got = jnp.where(high == h, piece, got)
        out_ref[a, :width, :] = got * meta_ref[3, row, :]
        out_ref[a, width:, :] = jnp.broadcast_to(meta_ref[2, row, :], (META, LANES))
        return carry

    lax.fori_loop(0, slabs, gather, 0)


def fluid_kernel(x_ref, diag_ref, left_ref, right_ref, got_ref, out_ref, lhs_ref, acc_ref):
    width, rows = x_ref.shape
    slabs = got_ref.shape[0]
    wide = 2 * LANES
    highs = rows // wide
    group = 4
    acc_ref[...] = jnp.zeros_like(acc_ref)

    def step(g, carry):
        ohs = []
        for s in range(group):
            a = g * group + s
            target = got_ref[a, width : width + 1, :].astype(jnp.int32)
            vals = got_ref[a, :width, :]
            hi = vals.astype(BF16).astype(F32)
            lo = vals - hi
            high = jnp.broadcast_to(target // wide, (width, LANES))
            low = target % wide
            at = s * wide
            for h in range(highs):
                hit = high == h
                lhs_ref[h * width : (h + 1) * width, at : at + LANES] = jnp.where(
                    hit, hi, 0.0
                ).astype(BF16)
                lhs_ref[h * width : (h + 1) * width, at + LANES : at + wide] = jnp.where(
                    hit, lo, 0.0
                ).astype(BF16)
            oh = jnp.where(
                lax.broadcasted_iota(jnp.int32, (wide, LANES), 0) == low, 1.0, 0.0
            ).astype(BF16)
            ohs += [oh, oh]
        acc_ref[...] += nt(lhs_ref[...], jnp.concatenate(ohs, axis=1))
        return carry

    lax.fori_loop(0, slabs // group, step, 0)
    lane = lax.broadcasted_iota(jnp.int32, (width, LANES), 1)
    pieces = rows // LANES
    for t in range(pieces):
        own = x_ref[:, t * LANES : (t + 1) * LANES]
        prev = left_ref[...] if t == 0 else x_ref[:, (t - 1) * LANES : t * LANES]
        nxt = right_ref[...] if t == pieces - 1 else x_ref[:, (t + 1) * LANES : (t + 2) * LANES]
        before = jnp.where(lane == 0, pltpu.roll(prev, 1, 1), pltpu.roll(own, 1, 1))
        after = jnp.where(
            lane == LANES - 1, pltpu.roll(nxt, LANES - 1, 1), pltpu.roll(own, LANES - 1, 1)
        )
        h, side = t // 2, t % 2
        added = acc_ref[h * width : (h + 1) * width, side * LANES : (side + 1) * LANES]
        d = diag_ref[:, t * LANES : (t + 1) * LANES]
        out_ref[:, t * LANES : (t + 1) * LANES] = d * own - before - after + added


def face_kernel(y_ref, faces_ref, match_ref, weight_ref, out_ref):
    width = y_ref.shape[0]
    rounds, face = match_ref.shape
    pieces = face // LANES
    for m in range(rounds):
        for o in range(pieces):
            index = match_ref[m : m + 1, o * LANES : (o + 1) * LANES]
            high = jnp.broadcast_to(index // LANES, (width, LANES))
            low = jnp.broadcast_to(index % LANES, (width, LANES))
            got = jnp.zeros((width, LANES), F32)
            for h in range(pieces):
                piece = lane_gather(faces_ref[m, :, h * LANES : (h + 1) * LANES], low)
                got = jnp.where(high == h, piece, got)
            at = m * face + o * LANES
            w = weight_ref[m : m + 1, o * LANES : (o + 1) * LANES]
            out_ref[:, at : at + LANES] = y_ref[:, at : at + LANES] + w * got
    done = rounds * face
    if done < y_ref.shape[1]:
        out_ref[:, done:] = y_ref[:, done:]


def call(kernel, out_shape, *args, scratch=()):
    return pl.pallas_call(
        kernel,
        out_shape=out_shape,
        in_specs=[pl.BlockSpec(memory_space=pltpu.VMEM)] * len(args),
        out_specs=pl.BlockSpec(memory_space=pltpu.VMEM),
        scratch_shapes=list(scratch),
        compiler_params=pltpu.CompilerParams(vmem_limit_bytes=40 << 20),
    )(*args)


def swapped(block, axis, bit):
    count = lax.axis_size(axis)
    route = []
    for low in range(count):
        high = low | 1 << bit
        if high != low and high < count:
            route += [(low, high), (high, low)]
    return lax.ppermute(block, axis, route)


def shards(
    current, prior, block_values, block_cols, face_match, face_weight,
    fluid_diag, wet_source, wet_dest, wet_target, wet_weight,
):
    high = lax.Precision.HIGH
    width, local_rows = current.shape
    face_rows = face_match.shape[2]
    row_blocks = block_cols.shape[0]
    wet_slots = wet_source.shape[0]
    grp, dev = lax.axis_size("grp"), lax.axis_size("dev")
    subdomains = grp * dev
    total_rows = local_rows * lax.axis_size("sec") * subdomains
    capacity = 2 * wet_slots // subdomains + 8
    per = -(-capacity // LANES)
    slabs = subdomains * per
    is_shell = lax.axis_index("sec") == 0
    flat_prior = prior.reshape(-1, local_rows)
    basis = flat_prior.shape[0]
    cross = lax.psum(
        lax.dot_general(flat_prior, flat_prior, NT, precision=high), ALL
    )
    faces = []
    for sweep in range(ROUNDS):
        face_now = current[:, sweep * face_rows : (sweep + 1) * face_rows]
        if sweep < 2:
            faces.append(swapped(face_now, "dev", sweep))
        else:
            faces.append(swapped(face_now, "grp", sweep - 2))
    up = [(i, i + 1) for i in range(subdomains - 1)]
    down = [(j, i) for i, j in up]
    left = lax.ppermute(current[:, -LANES:], ("grp", "dev"), up)
    right = lax.ppermute(current[:, :LANES], ("grp", "dev"), down)
    tiled = (wet_slots // LANES, LANES)

    def pack(x):
        return call(
            functools.partial(pack_kernel, subdomains, per),
            jax.ShapeDtypeStruct((slabs, width + META, LANES), F32),
            x, wet_source.reshape(tiled), wet_dest.reshape(tiled), wet_target.reshape(tiled),
            wet_weight.reshape(tiled), scratch=[pltpu.VMEM((4, slabs, LANES), F32)],
        )

    packed = lax.cond(
        is_shell, pack, lambda x: jnp.zeros((slabs, width + META, LANES), F32), current
    )
    both = jnp.concatenate([jnp.zeros_like(packed), packed], axis=0)
    got = lax.all_to_all(both, ALL, split_axis=0, concat_axis=0, tiled=True)[:slabs]

    def shell_apply(vector):
        picked = vector.reshape(width, row_blocks, BS)[:, block_cols, :]
        matrices = block_values.reshape(row_blocks, NB, BS, BS)
        result = jnp.einsum("kibc,ibrc->kir", picked, matrices, precision=high)
        return call(
            face_kernel, jax.ShapeDtypeStruct((width, local_rows), F32),
            result.reshape(width, local_rows), jnp.stack(faces), face_match[0], face_weight[0],
        )

    def fluid_apply(vector):
        return call(
            fluid_kernel, jax.ShapeDtypeStruct((width, local_rows), F32),
            vector, fluid_diag[None, :], left, right, got,
            scratch=[
                pltpu.VMEM((local_rows // 256 * width, 8 * LANES), BF16),
                pltpu.VMEM((local_rows // 256 * width, 2 * LANES), F32),
            ],
        )

    image = lax.cond(is_shell, shell_apply, fluid_apply, current)
    highest = lax.Precision.HIGHEST
    local = jnp.concatenate(
        [
            lax.dot_general(flat_prior, image, NT, precision=high),
            lax.dot_general(image, image, NT, precision=high),
        ],
        axis=0,
    )
    summed = lax.psum(local, ALL)
    first, square = summed[:basis], summed[basis:]
    coef = 2.0 * first - jnp.dot(cross, first, precision=highest)
    inner = lax.dot_general(coef, first, (((0,), (0,)), ((), ())), precision=highest)
    outer = lax.dot_general(
        coef, jnp.dot(cross, coef, precision=highest), (((0,), (0,)), ((), ())), precision=highest
    )
    gram = (square - inner - inner.T + outer) / total_rows
    factor = jnp.linalg.cholesky(gram)
    inverse = lax.linalg.triangular_solve(
        factor, jnp.eye(width, dtype=F32), left_side=True, lower=True
    )
    mix = -lax.dot_general(inverse, coef, (((1,), (1,)), ((), ())), precision=highest)
    next_block = jnp.dot(inverse, image, precision=high) + jnp.dot(mix, flat_prior, precision=high)
    return (next_block, coef.reshape(prior.shape[0], width, width), factor.T)


def solution(mesh):
    placed = (
        P(None, ALL),
        P(None, None, ALL),
        P(("grp", "dev"), None, None),
        P(("grp", "dev"), None),
        P(("grp", "dev"), None, None),
        P(("grp", "dev"), None, None),
        P(("grp", "dev")),
        P(("grp", "dev")),
        P(("grp", "dev"), None),
        P(("grp", "dev")),
        P(("grp", "dev")),
    )
    return jax.shard_map(
        shards, mesh=mesh, in_specs=placed, out_specs=(P(None, ALL), P(), P()), check_vma=False
    )
```

time: 435 us -> 254 us (0.58); the launches traced: 428 us -> 254 us
  blocking collectives: 153 us -> 39.4 us
  other arithmetic: 51 us -> 7.69 us
  local copies, waits for them, and re-layouts: 67.1 us -> 27.5 us
  matrix products: 76.7 us -> 37.5 us
  waiting for transfers between devices: 48.2 us -> 81.5 us
  Pallas kernels: 0 us -> 27 us
  between operations: 1.34 us -> 14.3 us
  loops' own time: 7.2 us -> 0.53 us
  starting transfers between devices: 24 us -> 18.3 us
    psum x3 -> x1, blocking collectives: 153 us -> 39.4 us  [shards(): summed = lax.psum(local, ALL)]
    ppermute x4, waiting for transfers between devices: 0.01 us -> 49.6 us  [swapped(): return lax.ppermute(block, axis, route)]
    ppermute x2, waiting for transfers between devices: 48.2 us -> 0.01 us  [the longest x1 0.01 us: shards(): left = lax.ppermute(current[:, -LANES:], ('grp', 'dev'), up)]
    dot_general x6 -> x11, matrix products: 75 us -> 37.3 us  [the longest x1 13.9 us: shell_apply(): result = jnp.einsum('kibc,ibrc->kir', picked, matrices, precision=high)]
    psum x0 -> x1, waiting for transfers between devices: none -> 31.8 us  [shards(): lax.psum(lax.dot_general(flat_prior, flat_prior, NT, precision=high), ALL)]
    pallas_call x0 -> x2, Pallas kernels: none -> 27 us  [call(): pl.pallas_call(kernel, out_shape=out_shape, in_specs=[pl.BlockSpec(memory...]
    unnamed x4 -> x0, other arithmetic: 22.4 us -> none
    unnamed x14 -> x12, local copies, waits for them, and re-layouts: 15.2 us -> 1.47 us
  transfers between devices with their start and end apart: 8 -> 8, of which waited for: 2 -> 3; matrix products, arithmetic and copies ran while one was open for 7% -> 21% of each run, Pallas kernels for 0% -> 1%
where the time goes in v1:
time: 254 us
  waiting for transfers between devices  81.5 us (32%)
  blocking collectives  39.4 us (16%)
  matrix products  37.5 us (15%)
  local copies, waits for them, and re-layouts  27.5 us (11%)
  Pallas kernels  27 us (11%)
  starting transfers between devices  18.3 us (7%)
  between operations  14.3 us (6%)
  other arithmetic  7.69 us (3%)
    ppermute x4, waiting for transfers between devices, swapped(): return lax.ppermute(block, axis, route)  49.6 us
    psum x1, blocking collectives, shards(): summed = lax.psum(local, ALL)  39.4 us
    psum x1, waiting for transfers between devices, shards(): lax.psum(lax.dot_general(flat_prior, flat_prior, NT, precision=high), ALL)  31.8 us
    pallas_call x2, Pallas kernels, call(): pl.pallas_call(kernel, out_shape=out_shape, in_specs=[pl.BlockSpec(memory...  27 us
    reshape x1, local copies, waits for them, and re-layouts, shell_apply(): matrices = block_values.reshape(row_blocks, NB, BS, BS)  17.9 us
    dot_general x1, matrix products, shell_apply(): result = jnp.einsum('kibc,ibrc->kir', picked, matrices, precision=high)  13.9 us
    dot_general x1, matrix products, shards(): lax.dot_general(flat_prior, flat_prior, NT, precision=high)  8.13 us
    all_to_all x1, starting transfers between devices, shards(): lax.all_to_all(both, ALL, split_axis=0, concat_axis=0, tiled=True)[:slabs]  7.47 us
  transfers between devices with their start and end apart: 8, of which 3 were waited for; matrix products, arithmetic and copies ran while one was open for 21% of the time, Pallas kernels for 1%

profile of v1, /device:TPU:0, one launch (start us, length us, event | category | flops | bytes accessed | tf_op | source)
XLA Modules:
  0.0 253.6 jit_solution(18224657557040044086)
XLA Ops:
  7.2 24.3 %conditional.2 = (f32[64,40,128]{2,1,0:T(8,128)S(1)}) conditional(s32[]{:T(128)} %convert_element_type.2, () %tuple.20, (s32[3072]{0:T(1024)}, s32[3072,1]{0,1:T(1,128)}, s32[3072]{0:T(1024)}, f32[3072]{0:T(1024)}, f32[32,6144]{1,0:T(8,128)}) %tuple.21), branch_computations={%region_0.0_spmd, %region_1.0_spmd} | conditional | bytes 1310732 | solution.py:232
  7.2 24.3 %branch_1_fun.2 = f32[64,40,128]{2,1,0:T(8,128)S(1)} custom-call(f32[32,6144]{1,0:T(8,128)} %get-tuple-element.27.x_ref, s32[24,128]{1,0:T(8,128)} %bitcast.68, s32[24,128]{1,0:T(8,128)} %bitcast.69, s32[24,128]{1,0:T(8,128)} %bitcast.70, f32[24,128]{1,0:T(8,128)} %bitcast.71), custom_call_target="tpu_custom_call" | custom-call | tf_op jit(solution)/shard_map/cond/branch_1_fun/pallas_call | solution.py:170
  31.5 1.7 concatenate.6
  33.2 7.5 %all-to-all-start = ((f32[128,40,128]{2,1,0:T(8,128)}), f32[128,40,128]{2,1,0:T(8,128)}, u32[]{:S(2)}, u32[]{:S(2)}) async-start(f32[128,40,128]{2,1,0:T(8,128)} %concatenate.6), calls=%async_computation | async-start | bytes 5242880 | tf_op jit(solution)/shard_map/all_to_all | solution.py:236
  40.7 0.0 all-reduce.3.cloned.1.call-start
  40.7 0.1 fusion.14
  40.8 1.8 collective-permute-start.2
  42.6 2.4 collective-permute-start.3
  45.0 1.5 collective-permute-start.4
  46.5 1.5 collective-permute-start.5
  48.0 2.4 collective-permute-start
  50.3 38.6 %collective-permute-done.2 = f32[32,1536]{1,0:T(8,128)} collective-permute-done((f32[32,1536]{1,0:T(8,128)S(1)}, f32[32,1536]{1,0:T(8,128)}, u32[]{:S(2)}, u32[]{:S(2)}) %collective-permute-start.2) | collective-permute-done | bytes 196640 | tf_op jit(solution)/shard_map/ppermute | solution.py:187
  88.9 1.3 collective-permute-start.1
  90.2 8.1 %fusion.17 = f32[256,256]{1,0:T(8,128)} fusion(f32[256,6144]{1,0:T(8,128)} %bitcast.57), kind=kOutput, calls=%fused_computation.33 | convolution fusion | flops 2415919104 | bytes 6553600 | tf_op jit(solution)/shard_map/dot_general | solution.py:209
  98.4 0.0 all-reduce.3.cloned.1.call-update
  98.4 11.1 %collective-permute-done.3 = f32[32,1536]{1,0:T(8,128)S(1)} collective-permute-done((f32[32,1536]{1,0:T(8,128)S(1)}, f32[32,1536]{1,0:T(8,128)S(1)}, u32[]{:S(2)}, u32[]{:S(2)}) %collective-permute-start.3) | collective-permute-done | bytes 196640 | tf_op jit(solution)/shard_map/ppermute | solution.py:187
  109.5 42.2 %conditional.3 = (f32[32,6144]{1,0:T(8,128)S(1)}) conditional(s32[]{:T(128)} %convert_element_type.2, (f32[6144]{0:T(1024)S(1)}, f32[32,6144]{1,0:T(8,128)S(1)}, f32[32,128]{1,0:T(8,128)S(1)}, f32[32,128]{1,0:T(8,128)S(1)}, f32[128,40,128]{2,1,0:T(8,128)}) %tuple.44, (f32[32,6144]{1,0:T(8,128)S(1)}, s32[64,6]{0,1:T(8,128)S(1)}, ...), branch_computations={%region_2.0_spmd, %region_3.0_spmd} | conditional | flops 680069248 | bytes 70009008 | solution.py:257
  109.8 17.9 %reshape.38 = f32[64,6,96,96]{3,2,0,1:T(8,128)} reshape(f32[64,6,9216]{2,0,1:T(8,128)} %get-tuple-element.82) | data formatting | bytes 28311552 | tf_op jit(solution)/shard_map/cond/branch_1_fun/reshape | solution.py:240
  127.6 0.4 reshape.37
  128.1 0.6 copy.39
  128.7 0.1 copy.42
  128.8 0.1 reshape.46
  128.9 3.8 %gather_fusion = f32[384,32,96]{2,1,0:T(8,128)} fusion(f32[32,64,96]{2,0,1:T(8,128)S(1)} %copy.39, s32[1024]{0:T(1024)S(1)} %pad_clamp_fusion), kind=kCustom, calls=%fused_computation | custom fusion | bytes 9438720 | tf_op jit(solution)/shard_map/cond/branch_1_fun/gather | solution.py:239
  132.7 13.9 %fusion.2 = f32[32,64,96]{2,0,1:T(8,128)S(1)} fusion(f32[32,64,6,96]{3,0,2,1:T(8,128)} %bitcast.60, f32[64,6,96,96]{3,2,0,1:T(8,128)} %reshape.38), kind=kOutput, calls=%fused_computation.3 | convolution fusion | flops 679477248 | bytes 19660800 | tf_op jit(solution)/shard_map/cond/branch_1_fun/kibc,ibrc->kir/dot_general | solution.py:241
  146.6 0.6 copy.41
  147.2 0.6 reshape.39.y_ref
  147.9 1.0 pad_maximum_fusion.faces_ref
  148.9 2.7 %branch_1_fun.3 = f32[32,6144]{1,0:T(8,128)S(1)} custom-call(f32[32,6144]{1,0:T(8,128)S(1)} %reshape.39.y_ref, f32[4,32,1536]{2,1,0:T(8,128)S(1)} %pad_maximum_fusion.faces_ref, s32[4,1536]{1,0:T(4,128)S(1)} %bitcast.66, f32[4,1536]{1,0:T(4,128)S(1)} %bitcast.67), custom_call_target="tpu_custom_call" | custom-call | tf_op jit(solution)/shard_map/cond/branch_1_fun/pallas_call | solution.py:170
  151.7 5.6 %convolution_bitcast_fusion = f32[256,32]{0,1:T(8,128)S(1)} fusion(f32[32,6144]{1,0:T(8,128)S(1)} %get-tuple-element.130, f32[256,6144]{1,0:T(8,128)} %bitcast.58), kind=kOutput, calls=%fused_computation.10 | convolution fusion | flops 301989888 | bytes 7110656 | tf_op jit(solution)/shard_map/dot_general | solution.py:261
  157.4 0.5 fusion.16
  157.8 39.4 %psum.14 = f32[288,32]{0,1:T(8,128)S(1)} all-reduce(f32[288,32]{0,1:T(8,128)S(1)} %pad_maximum_fusion.1), channel_id=1, replica_groups=mesh['sec'=2,'grp'=4,'dev'=4] {'sec','grp','dev'}, use_global_device_ids=true, to_apply=%region_4.0 | all-reduce | flops 9216 | bytes 73728 | tf_op jit(solution)/shard_map/psum | solution.py:266
  197.2 31.8 %all-reduce.3.cloned.1.call-done = f32[256,256]{1,0:T(8,128)} async-done(((f32[256,256]{1,0:T(8,128)}), f32[256,256]{1,0:T(8,128)}) %all-reduce.3.cloned.1.call-update) | async-done | bytes 262160 | tf_op jit(solution)/shard_map/psum | solution.py:208
  229.0 1.3 convolution_subtract_fusion
  230.3 0.2 fusion.7
  230.5 0.8 copy.50
  231.3 0.1 copy.43
  231.3 1.3 fusion.18
  232.6 0.2 fusion.5
  232.8 0.1 copy.45
  232.9 2.9 %cholesky.17 = f32[32,32]{1,0:T(8,128)S(1)} custom-call(f32[32,32]{1,0:T(8,128)S(1)} %fusion.12), custom_call_target="Cholesky" | custom-call | tf_op jit(solution)/shard_map/jit(cholesky)/cholesky | solution.py:274
  235.8 0.6 compare_reduce_fusion
  236.5 0.7 fusion.13
  237.1 2.4 custom-call.6
  239.6 0.2 fusion.10
  239.8 0.2 convolution_negate_fusion
  240.0 4.7 %fusion.19 = f32[32,6144]{1,0:T(8,128)S(1)} fusion(f32[32,256]{1,0:T(8,128)S(1)} %convolution_negate_fusion, f32[256,6144]{1,0:T(8,128)} %bitcast.59), kind=kOutput, calls=%fused_computation.35 | convolution fusion | flops 301989888 | bytes 7110656 | tf_op jit(solution)/shard_map/dot_general | solution.py:279
  244.7 1.3 convolution_add_fusion
  246.1 0.7 copy.47
  (33 shorter events, 0.1 us)
Async XLA Ops:
  31.5 9.2 %copy-start = (f32[32,6144]{1,0:T(8,128)S(1)}, f32[32,6144]{1,0:T(8,128)}, u32[]{:S(2)}) copy-start(f32[32,6144]{1,0:T(8,128)} %param.15) | copy-start | bytes 2359300
  33.2 76.3 %all-to-all-start = ((f32[128,40,128]{2,1,0:T(8,128)}), f32[128,40,128]{2,1,0:T(8,128)}, u32[]{:S(2)}, u32[]{:S(2)}) async-start(f32[128,40,128]{2,1,0:T(8,128)} %concatenate.6), calls=%async_computation | async-start | bytes 5242880 | tf_op jit(solution)/shard_map/all_to_all | solution.py:236
  40.7 188.4 %all-reduce.3.cloned.1.call-start = ((), (), s32[]{:S(2)}) async-start(), calls=%async_computation.1 | async-start | bytes 524288 | tf_op jit(solution)/shard_map/psum | solution.py:208
  40.8 48.1 %collective-permute-start.2 = (f32[32,1536]{1,0:T(8,128)S(1)}, f32[32,1536]{1,0:T(8,128)}, u32[]{:S(2)}, u32[]{:S(2)}) collective-permute-start(f32[32,1536]{1,0:T(8,128)S(1)} %get-tuple-element.124), channel_id=1, source_target_pairs={{0,1},{1,0},{2,3},{3,2},{4,5},{5,4},{6,7},{7,6},{8,9},{9,8},{10,11... | collective-permute-start | bytes 589832 | tf_op jit(solution)/shard_map/ppermute | solution.py:187
  42.6 66.9 %collective-permute-start.3 = (f32[32,1536]{1,0:T(8,128)S(1)}, f32[32,1536]{1,0:T(8,128)S(1)}, u32[]{:S(2)}, u32[]{:S(2)}) collective-permute-start(f32[32,1536]{1,0:T(8,128)S(1)} %get-tuple-element.123), channel_id=1, source_target_pairs={{0,2},{2,0},{1,3},{3,1},{4,6},{6,4},{5,7},{7,5},{8,10},{10,8},{9,1... | collective-permute-start | bytes 589832 | tf_op jit(solution)/shard_map/ppermute | solution.py:187
  45.0 64.5 %collective-permute-start.4 = (f32[32,1536]{1,0:T(8,128)S(1)}, f32[32,1536]{1,0:T(8,128)S(1)}, u32[]{:S(2)}, u32[]{:S(2)}) collective-permute-start(f32[32,1536]{1,0:T(8,128)S(1)} %get-tuple-element.122), channel_id=1, source_target_pairs={{0,4},{4,0},{8,12},{12,8},{1,5},{5,1},{9,13},{13,9},{2,6},{6,2},{1... | collective-permute-start | bytes 589832 | tf_op jit(solution)/shard_map/ppermute | solution.py:187
  46.5 63.0 %collective-permute-start.5 = (f32[32,1536]{1,0:T(8,128)S(1)}, f32[32,1536]{1,0:T(8,128)S(1)}, u32[]{:S(2)}, u32[]{:S(2)}) collective-permute-start(f32[32,1536]{1,0:T(8,128)S(1)} %get-tuple-element.121), channel_id=1, source_target_pairs={{0,8},{8,0},{4,12},{12,4},{1,9},{9,1},{5,13},{13,5},{2,10},{10,2},... | collective-permute-start | bytes 589832 | tf_op jit(solution)/shard_map/ppermute | solution.py:187
  48.0 61.5 %collective-permute-start = (f32[32,128]{1,0:T(8,128)S(1)}, f32[32,128]{1,0:T(8,128)S(1)}, u32[]{:S(2)}, u32[]{:S(2)}) collective-permute-start(f32[32,128]{1,0:T(8,128)S(1)} %get-tuple-element.126), channel_id=1, source_target_pairs={{0,1},{1,2},{2,3},{3,4},{4,5},{5,6},{6,7},{7,8},{8,9},{9,10},{10,1... | collective-permute-start | bytes 49160 | tf_op jit(solution)/shard_map/ppermute | solution.py:220
  88.9 20.6 %collective-permute-start.1 = (f32[32,128]{1,0:T(8,128)S(1)}, f32[32,128]{1,0:T(8,128)S(1)}, u32[]{:S(2)}, u32[]{:S(2)}) collective-permute-start(f32[32,128]{1,0:T(8,128)S(1)} %get-tuple-element.125), channel_id=1, source_target_pairs={{1,0},{2,1},{3,2},{4,3},{5,4},{6,5},{7,6},{8,7},{9,8},{10,9},{11,1... | collective-permute-start | bytes 49160 | tf_op jit(solution)/shard_map/ppermute | solution.py:221
  90.2 19.3 %copy-start.7 = (f32[6144]{0:T(1024)S(1)}, f32[6144]{0:T(1024)}, u32[]{:S(2)}) copy-start(f32[6144]{0:T(1024)} %param.21) | copy-start | bytes 73732
  90.2 19.3 %copy-start.8 = (s32[1,4,1536]{2,1,0:T(4,128)S(1)}, s32[1,4,1536]{2,1,0:T(4,128)}, u32[]{:S(2)}) copy-start(s32[1,4,1536]{2,1,0:T(4,128)} %param.19) | copy-start | bytes 73732
  90.2 19.3 %copy-start.9 = (f32[1,4,1536]{2,1,0:T(4,128)S(1)}, f32[1,4,1536]{2,1,0:T(4,128)}, u32[]{:S(2)}) copy-start(f32[1,4,1536]{2,1,0:T(4,128)} %param.20) | copy-start | bytes 73732
  90.2 19.3 %copy-start.10 = (s32[64,6]{0,1:T(8,128)S(1)}, s32[64,6]{0,1:T(8,128)}, u32[]{:S(2)}) copy-start(s32[64,6]{0,1:T(8,128)} %param.18) | copy-start | bytes 4612
  109.7 17.9 %copy-start.1 = (f32[32,1536]{1,0:T(8,128)}, f32[32,1536]{1,0:T(8,128)S(1)}, u32[]{:S(2)}) copy-start(f32[32,1536]{1,0:T(8,128)S(1)} %get-tuple-element.58) | copy-start | bytes 589828 | tf_op jit(solution)/shard_map/cond
  109.7 17.9 %copy-start.3 = (f32[32,1536]{1,0:T(8,128)}, f32[32,1536]{1,0:T(8,128)S(1)}, u32[]{:S(2)}) copy-start(f32[32,1536]{1,0:T(8,128)S(1)} %get-tuple-element.59) | copy-start | bytes 589828 | tf_op jit(solution)/shard_map/cond
  109.8 17.9 %copy-start.5 = (f32[32,1536]{1,0:T(8,128)}, f32[32,1536]{1,0:T(8,128)S(1)}, u32[]{:S(2)}) copy-start(f32[32,1536]{1,0:T(8,128)S(1)} %get-tuple-element.60) | copy-start | bytes 589828 | tf_op jit(solution)/shard_map/cond
  132.7 15.1 %copy-start.2 = (f32[32,1536]{1,0:T(8,128)S(1)}, f32[32,1536]{1,0:T(8,128)}, u32[]{:S(2)}) copy-start(f32[32,1536]{1,0:T(8,128)} %copy-done.1) | copy-start | bytes 589828 | tf_op jit(solution)/shard_map/cond
  132.7 15.1 %copy-start.4 = (f32[32,1536]{1,0:T(8,128)S(1)}, f32[32,1536]{1,0:T(8,128)}, u32[]{:S(2)}) copy-start(f32[32,1536]{1,0:T(8,128)} %copy-done.3) | copy-start | bytes 589828 | tf_op jit(solution)/shard_map/cond
  132.7 15.1 %copy-start.6 = (f32[32,1536]{1,0:T(8,128)S(1)}, f32[32,1536]{1,0:T(8,128)}, u32[]{:S(2)}) copy-start(f32[32,1536]{1,0:T(8,128)} %copy-done.5) | copy-start | bytes 589828 | tf_op jit(solution)/shard_map/cond
Sparse Core Ops, SparseCore 0:
  98.5 130.4 all-reduce.2

commit v2 on v1

--- a/solution.py
+++ b/solution.py
@@ -166,25 +166,270 @@
         out_ref[:, done:] = y_ref[:, done:]
 
 
-def call(kernel, out_shape, *args, scratch=()):
+MESH = pl.DeviceIdType.MESH
+
+
+def place(index):
+    dev = lax.axis_size("dev")
+    grp = lax.axis_size("grp")
+    return (index // (grp * dev), index // dev % grp, index % dev)
+
+
+def own_index():
+    grp, dev = lax.axis_size("grp"), lax.axis_size("dev")
+    return (lax.axis_index("sec") * grp + lax.axis_index("grp")) * dev + lax.axis_index("dev")
+
+
+def everyone(me, n, body):
+    def step(s, carry):
+        body(lax.rem(me + s, n))
+        return carry
+
+    lax.fori_loop(1, n, step, 0)
+
+
+def announce(me, n):
+    barrier = pltpu.get_barrier_semaphore()
+    everyone(
+        me, n,
+        lambda d: pl.semaphore_signal(barrier, inc=1, device_id=place(d), device_id_type=MESH),
+    )
+    return barrier
+
+
+def remote(src, dst, send, recv, device):
+    return pltpu.make_async_remote_copy(
+        src_ref=src, dst_ref=dst, send_sem=send, recv_sem=recv, device_id=device,
+        device_id_type=MESH,
+    )
+
+
+class Summing:
+    def __init__(self, me, n, stage, slots, total, sems):
+        self.me, self.n = me, n
+        self.stage, self.slots, self.total, self.sems = stage, slots, total, sems
+
+    def piece(self, to, at):
+        return remote(
+            self.stage.at[to], self.slots.at[at], self.sems.at[0, to], self.sems.at[1, at],
+            place(to),
+        )
+
+    def whole(self, to, at):
+        return remote(
+            self.total.at[at], self.total.at[at], self.sems.at[2, to], self.sems.at[3, at],
+            place(to),
+        )
+
+    def scatter(self):
+        everyone(self.me, self.n, lambda d: self.piece(d, self.me).start())
+
+    def gather(self):
+        me = self.me
+        everyone(me, self.n, lambda d: self.piece(d, d).wait_recv())
+        self.slots[me] = self.stage[me]
+        self.total[me] = jnp.sum(self.slots[...], axis=0)
+        everyone(me, self.n, lambda d: self.whole(d, me).start())
+
+    def finish(self):
+        everyone(self.me, self.n, lambda d: self.whole(d, d).wait_recv())
+        everyone(self.me, self.n, lambda d: self.piece(d, d).wait_send())
+        everyone(self.me, self.n, lambda d: self.whole(d, self.me).wait_send())
+
+
+def exchange_kernel(
+    subdomains, per, face, x_ref, pack_ref, prior_ref, cross_ref, faces_ref, edge_ref, got_ref,
+    stage, slots, total, sems, face_sems, edge_sems, wet_sems,
+):
+    n = 2 * subdomains
+    me = own_index()
+    sec, g, d = lax.axis_index("sec"), lax.axis_index("grp"), lax.axis_index("dev")
+    mine = lax.rem(me, subdomains)
+    rows = x_ref.shape[1]
+    partners = [
+        (0, g, d + 1 - 2 * lax.rem(d, 2)),
+        (0, g, d + 2 - 4 * lax.rem(d // 2, 2)),
+        (0, g + 1 - 2 * lax.rem(g, 2), d),
+        (0, g + 2 - 4 * lax.rem(g // 2, 2), d),
+    ]
+
+    def face_copy(m):
+        return remote(
+            x_ref.at[:, pl.ds(m * face, face)], faces_ref.at[m], face_sems.at[0, m],
+            face_sems.at[1, m], partners[m],
+        )
+
+    def edge_copy(side):
+        to = subdomains + lax.rem(mine + (1 if side == 0 else subdomains - 1), subdomains)
+        at = rows - LANES if side == 0 else 0
+        return remote(
+            x_ref.at[:, pl.ds(at, LANES)], edge_ref.at[side], edge_sems.at[0, side],
+            edge_sems.at[1, side], place(to),
+        )
+
+    def wet_copy(to, at):
+        return remote(
+            pack_ref.at[pl.ds(to * per, per)], got_ref.at[pl.ds(at * per, per)],
+            wet_sems.at[0, to], wet_sems.at[1, at], place(subdomains + to),
+        )
+
+    def each(body):
+        def step(s, carry):
+            body(lax.rem(mine + s, subdomains))
+            return carry
+
+        lax.fori_loop(0, subdomains, step, 0)
+
+    pl.semaphore_wait(announce(me, n), n - 1)
+
+    @pl.when(sec == 0)
+    def _():
+        for m in range(ROUNDS):
+            face_copy(m).start()
+        each(lambda q: wet_copy(q, mine).start())
+
+    @pl.when(sec == 1)
+    def _():
+        edge_copy(0).start()
+        edge_copy(1).start()
+
+    basis = prior_ref.shape[0]
+    chunk = 1024
+
+    def product(i, carry):
+        same, mixed = carry
+        hi, lo = split2(prior_ref[:, pl.ds(pl.multiple_of(i * chunk, chunk), chunk)])
+        return same + nt(hi, hi), mixed + nt(hi, lo)
+
+    zero = jnp.zeros((basis, basis), F32)
+    same, mixed = lax.fori_loop(0, rows // chunk, product, (zero, zero))
+    part = same + mixed + mixed.T
+    piece = basis // n
+    stage[...] = part.reshape(n, piece, basis)
+    summing = Summing(me, n, stage, slots, total, sems)
+    summing.scatter()
+    summing.gather()
+    summing.finish()
+    cross_ref[...] = total[...].reshape(basis, basis)
+
+    @pl.when(sec == 0)
+    def _():
+        for m in range(ROUNDS):
+            face_copy(m).wait()
+        each(lambda q: wet_copy(q, mine).wait_send())
+
+    @pl.when(sec == 1)
+    def _():
+        edge_copy(0).wait()
+        edge_copy(1).wait()
+        each(lambda q: wet_copy(q, q).wait_recv())
+
+
+def finish_kernel(
+    subdomains, total_rows, image_ref, prior_ref, cross_ref, next_ref, coef_ref, fac_ref,
+    high_ref, low_ref, stage, slots, total, sems,
+):
+    n = 2 * subdomains
+    me = own_index()
+    width, rows = image_ref.shape
+    basis = prior_ref.shape[0]
+    chunk = 1024
+    barrier = announce(me, n)
+
+    def product(i, carry):
+        head, square = carry
+        at = pl.ds(pl.multiple_of(i * chunk, chunk), chunk)
+        hi, lo = split2(prior_ref[:, at])
+        high_ref[:, at] = hi
+        low_ref[:, at] = lo
+        ih, il = split2(image_ref[:, at])
+        both = nt(jnp.concatenate([ih, il], axis=0), hi)
+        head = head + both[:width] + both[width:] + nt(ih, lo)
+        mixed = nt(ih, il)
+        square = square + nt(ih, ih) + mixed + mixed.T
+        return head, square
+
+    head, square = lax.fori_loop(
+        0, rows // chunk, product,
+        (jnp.zeros((width, basis), F32), jnp.zeros((width, width), F32)),
+    )
+    part = jnp.concatenate(
+        [head, square, jnp.zeros((width, -(basis + width) % LANES), F32)], axis=1
+    )
+    cuts = n // width
+    span = part.shape[1] // cuts
+    for i in range(n):
+        row, cut = i // cuts, i % cuts
+        stage[i] = part[row : row + 1, cut * span : (cut + 1) * span]
+    pl.semaphore_wait(barrier, n - 1)
+    summing = Summing(me, n, stage, slots, total, sems)
+    summing.scatter()
+    summing.gather()
+    summing.finish()
+    lines = [
+        jnp.concatenate([total[r * cuts + c] for c in range(cuts)], axis=1) if cuts > 1 else total[r]
+        for r in range(width)
+    ]
+    summed = jnp.concatenate(lines, axis=0)
+    first = summed[:, :basis]
+    square = summed[:, basis : basis + width]
+    cross = cross_ref[...]
+    highest = lax.Precision.HIGHEST
+
+    def dot(a, b):
+        return jnp.dot(a, b, precision=highest, preferred_element_type=F32)
+
+    def dot_nt(a, b):
+        return lax.dot_general(a, b, NT, precision=highest, preferred_element_type=F32)
+
+    coef = 2.0 * first - dot(first, cross)
+    gram = (
+        square - dot_nt(coef, first) - dot_nt(first, coef) + dot_nt(dot(coef, cross), coef)
+    ) * (1.0 / total_rows)
+    coef_ref[...] = coef.T
+    sub = lax.broadcasted_iota(jnp.int32, (width, 2 * width), 0)
+    lane = lax.broadcasted_iota(jnp.int32, (width, 2 * width), 1)
+    eye = jnp.where(sub + width == lane, 1.0, 0.0)
+    work = jnp.concatenate([gram, jnp.zeros((width, width), F32)], axis=1) + eye
+    for j in range(width):
+        root = jnp.sqrt(work[j : j + 1, j : j + 1])
+        row = work[j : j + 1, :] / root
+        column = work[:, j : j + 1] / root
+        work = jnp.where(sub == j, row, jnp.where(sub > j, work - column * row, work))
+    fac_ref[...] = jnp.where(sub <= lane, work, 0.0)[:, :width]
+    inverse = work[:, width:]
+    mix = -dot(inverse, coef)
+    vh, vl = split2(inverse)
+    mh, ml = split2(mix)
+    vs = jnp.concatenate([vh, vl], axis=0)
+    ms = jnp.concatenate([mh, ml], axis=0)
+
+    def out(i, carry):
+        at = pl.ds(pl.multiple_of(i * chunk, chunk), chunk)
+        ih, il = split2(image_ref[:, at])
+        a = jnp.dot(ms, high_ref[:, at], preferred_element_type=F32)
+        a = a + jnp.dot(vs, ih, preferred_element_type=F32)
+        c = jnp.dot(mh, low_ref[:, at], preferred_element_type=F32)
+        c = c + jnp.dot(vh, il, preferred_element_type=F32)
+        next_ref[:, at] = a[:width] + a[width:] + c
+        return carry
+
+    lax.fori_loop(0, rows // chunk, out, 0)
+
+
+def call(kernel, out_shape, *args, scratch=(), ident=None):
+    multi = isinstance(out_shape, (list, tuple))
+    spec = pl.BlockSpec(memory_space=pltpu.VMEM)
     return pl.pallas_call(
         kernel,
         out_shape=out_shape,
-        in_specs=[pl.BlockSpec(memory_space=pltpu.VMEM)] * len(args),
-        out_specs=pl.BlockSpec(memory_space=pltpu.VMEM),
+        in_specs=[spec] * len(args),
+        out_specs=tuple([spec] * len(out_shape)) if multi else spec,
         scratch_shapes=list(scratch),
-        compiler_params=pltpu.CompilerParams(vmem_limit_bytes=40 << 20),
+        compiler_params=pltpu.CompilerParams(
+            vmem_limit_bytes=40 << 20, collective_id=ident, has_side_effects=ident is not None
+        ),
     )(*args)
-
-
-def swapped(block, axis, bit):
-    count = lax.axis_size(axis)
-    route = []
-    for low in range(count):
-        high = low | 1 << bit
-        if high != low and high < count:
-            route += [(low, high), (high, low)]
-    return lax.ppermute(block, axis, route)
 
 
 def shards(
@@ -205,20 +450,6 @@
     is_shell = lax.axis_index("sec") == 0
     flat_prior = prior.reshape(-1, local_rows)
     basis = flat_prior.shape[0]
-    cross = lax.psum(
-        lax.dot_general(flat_prior, flat_prior, NT, precision=high), ALL
-    )
-    faces = []
-    for sweep in range(ROUNDS):
-        face_now = current[:, sweep * face_rows : (sweep + 1) * face_rows]
-        if sweep < 2:
-            faces.append(swapped(face_now, "dev", sweep))
-        else:
-            faces.append(swapped(face_now, "grp", sweep - 2))
-    up = [(i, i + 1) for i in range(subdomains - 1)]
-    down = [(j, i) for i, j in up]
-    left = lax.ppermute(current[:, -LANES:], ("grp", "dev"), up)
-    right = lax.ppermute(current[:, :LANES], ("grp", "dev"), down)
     tiled = (wet_slots // LANES, LANES)
 
     def pack(x):
@@ -232,8 +463,30 @@
     packed = lax.cond(
         is_shell, pack, lambda x: jnp.zeros((slabs, width + META, LANES), F32), current
     )
-    both = jnp.concatenate([jnp.zeros_like(packed), packed], axis=0)
-    got = lax.all_to_all(both, ALL, split_axis=0, concat_axis=0, tiled=True)[:slabs]
+    n = 2 * subdomains
+    cross, faces, edges, got = call(
+        functools.partial(exchange_kernel, subdomains, per, face_rows),
+        (
+            jax.ShapeDtypeStruct((basis, basis), F32),
+            jax.ShapeDtypeStruct((ROUNDS, width, face_rows), F32),
+            jax.ShapeDtypeStruct((2, width, LANES), F32),
+            jax.ShapeDtypeStruct(packed.shape, F32),
+        ),
+        current, packed, flat_prior,
+        scratch=[
+            pltpu.VMEM((n, basis // n, basis), F32),
+            pltpu.VMEM((n, basis // n, basis), F32),
+            pltpu.VMEM((n, basis // n, basis), F32),
+            pltpu.SemaphoreType.DMA((4, n)),
+            pltpu.SemaphoreType.DMA((2, ROUNDS)),
+            pltpu.SemaphoreType.DMA((2, 2)),
+            pltpu.SemaphoreType.DMA((2, subdomains)),
+        ],
+        ident=0,
+    )
+    mine = lax.axis_index("grp") * dev + lax.axis_index("dev")
+    left = jnp.where(mine == 0, 0.0, edges[0])
+    right = jnp.where(mine == subdomains - 1, 0.0, edges[1])
 
     def shell_apply(vector):
         picked = vector.reshape(width, row_blocks, BS)[:, block_cols, :]
@@ -241,7 +494,7 @@
         result = jnp.einsum("kibc,ibrc->kir", picked, matrices, precision=high)
         return call(
             face_kernel, jax.ShapeDtypeStruct((width, local_rows), F32),
-            result.reshape(width, local_rows), jnp.stack(faces), face_match[0], face_weight[0],
+            result.reshape(width, local_rows), faces, face_match[0], face_weight[0],
         )
 
     def fluid_apply(vector):
@@ -255,29 +508,26 @@
         )
 
     image = lax.cond(is_shell, shell_apply, fluid_apply, current)
-    highest = lax.Precision.HIGHEST
-    local = jnp.concatenate(
-        [
-            lax.dot_general(flat_prior, image, NT, precision=high),
-            lax.dot_general(image, image, NT, precision=high),
+    lanes = -(-(basis + width) // LANES) * LANES
+    cuts = n // width
+    piece = pltpu.VMEM((n, 1, lanes // cuts), F32)
+    next_block, coef, factor = call(
+        functools.partial(finish_kernel, subdomains, total_rows),
+        (
+            jax.ShapeDtypeStruct((width, local_rows), F32),
+            jax.ShapeDtypeStruct((basis, width), F32),
+            jax.ShapeDtypeStruct((width, width), F32),
+        ),
+        image, flat_prior, cross,
+        scratch=[
+            pltpu.VMEM((basis, local_rows), BF16),
+            pltpu.VMEM((basis, local_rows), BF16),
+            piece, piece, piece,
+            pltpu.SemaphoreType.DMA((4, n)),
         ],
-        axis=0,
-    )
-    summed = lax.psum(local, ALL)
-    first, square = summed[:basis], summed[basis:]
-    coef = 2.0 * first - jnp.dot(cross, first, precision=highest)
-    inner = lax.dot_general(coef, first, (((0,), (0,)), ((), ())), precision=highest)
-    outer = lax.dot_general(
-        coef, jnp.dot(cross, coef, precision=highest), (((0,), (0,)), ((), ())), precision=highest
-    )
-    gram = (square - inner - inner.T + outer) / total_rows
-    factor = jnp.linalg.cholesky(gram)
-    inverse = lax.linalg.triangular_solve(
-        factor, jnp.eye(width, dtype=F32), left_side=True, lower=True
-    )
-    mix = -lax.dot_general(inverse, coef, (((1,), (1,)), ((), ())), precision=highest)
-    next_block = jnp.dot(inverse, image, precision=high) + jnp.dot(mix, flat_prior, precision=high)
-    return (next_block, coef.reshape(prior.shape[0], width, width), factor.T)
+        ident=1,
+    )
+    return (next_block, coef.reshape(prior.shape[0], width, width), factor)
 
 
 def solution(mesh):

time: 254 us -> 146 us (0.57)
  waiting for transfers between devices: 81.5 us -> 0 us
  Pallas kernels: 27 us -> 98.3 us
  blocking collectives: 39.4 us -> 0 us
  matrix products: 37.5 us -> 13.9 us
  starting transfers between devices: 18.3 us -> 0 us
  between operations: 14.3 us -> 0.76 us
  other arithmetic: 7.69 us -> 0.01 us
  local copies, waits for them, and re-layouts: 27.5 us -> 31.6 us
    pallas_call x2 -> x4, Pallas kernels: 27 us -> 98.3 us  [call(): pl.pallas_call(kernel, out_shape=out_shape, in_specs=[spec] * len(args),...]
    ppermute x6 -> x0, waiting for transfers between devices: 49.6 us -> none  [the longest x4 49.6 us: swapped(): return lax.ppermute(block, axis, route)]
    psum x1 -> x0, blocking collectives: 39.4 us -> none  [shards(): summed = lax.psum(local, ALL)]
    psum x1 -> x0, waiting for transfers between devices: 31.8 us -> none  [shards(): lax.psum(lax.dot_general(flat_prior, flat_prior, NT, precision=high), ALL)]
    dot_general x10 -> x0, matrix products: 23.4 us -> none  [the longest x1 8.13 us: shards(): lax.dot_general(flat_prior, flat_prior, NT, precision=high)]
    ppermute x6 -> x0, starting transfers between devices: 10.8 us -> none  [the longest x4 7.16 us: swapped(): return lax.ppermute(block, axis, route)]
    all_to_all x1 -> x0, starting transfers between devices: 7.47 us -> none  [shards(): lax.all_to_all(both, ALL, split_axis=0, concat_axis=0, tiled=True)[:slabs]]
    another operation x5 -> x0, other arithmetic: 7.01 us -> none  [the longest x3 3.6 us: shards(): factor = jnp.linalg.cholesky(gram)]
  transfers between devices with their start and end apart: 8 -> 0, of which waited for: 3 -> 0; matrix products, arithmetic and copies ran while one was open for 21% -> 0% of each run, Pallas kernels for 1% -> 0%
where the time goes in v2:
time: 146 us; the launch traced here: 145 us
  Pallas kernels  98.3 us (67%)
  local copies, waits for them, and re-layouts  31.6 us (22%)
  matrix products  13.9 us (10%)
    pallas_call x4, Pallas kernels, call(): pl.pallas_call(kernel, out_shape=out_shape, in_specs=[spec] * len(args),...  98.3 us
    reshape x1, local copies, waits for them, and re-layouts, shell_apply(): matrices = block_values.reshape(row_blocks, NB, BS, BS)  17.6 us
    dot_general x1, matrix products, shell_apply(): result = jnp.einsum('kibc,ibrc->kir', picked, matrices, precision=high)  13.9 us
    unnamed x17, local copies, waits for them, and re-layouts  7.73 us
    gather x1, local copies, waits for them, and re-layouts, shell_apply(): picked = vector.reshape(width, row_blocks, BS)[:, block_cols, :]  3.75 us

profile of v2, /device:TPU:0, one launch (start us, length us, event | category | flops | bytes accessed | tf_op | source)
XLA Modules:
  0.0 144.8 jit_solution(15041252626917353572)
XLA Ops:
  0.6 0.0 copy-start.2
  0.6 0.0 copy-start.4
  0.7 0.0 copy-start.6
  0.7 0.0 copy-start.5
  0.7 0.0 copy-start.7
  0.7 24.4 %conditional.2 = (f32[64,40,128]{2,1,0:T(8,128)S(1)}) conditional(s32[]{:T(128)} %convert_element_type.4, () %tuple.20, (s32[3072]{0:T(1024)}, s32[3072,1]{0,1:T(1,128)}, s32[3072]{0:T(1024)}, f32[3072]{0:T(1024)}, f32[32,6144]{1,0:T(8,128)}) %tuple.21), branch_computations={%region_0.0_spmd, %region_1.0_spmd} | conditional | bytes 1310732 | solution.py:463
  0.7 24.4 %branch_1_fun.2 = f32[64,40,128]{2,1,0:T(8,128)S(1)} custom-call(f32[32,6144]{1,0:T(8,128)} %get-tuple-element.14.x_ref, s32[24,128]{1,0:T(8,128)} %bitcast.31, s32[24,128]{1,0:T(8,128)} %bitcast.32, s32[24,128]{1,0:T(8,128)} %bitcast.33, f32[24,128]{1,0:T(8,128)} %bitcast.34), custom_call_target="tpu_custom_call" | custom-call | tf_op jit(solution)/shard_map/cond/branch_1_fun/pallas_call | solution.py:423
  25.1 0.0 copy-start
  25.1 2.8 %copy-done = f32[8,32,6144]{2,1,0:T(8,128)S(1)} copy-done((f32[8,32,6144]{2,1,0:T(8,128)S(1)}, f32[8,32,6144]{2,1,0:T(8,128)}, u32[]{:S(2)}) %copy-start) | copy-done | bytes 6291480
  27.9 46.7 %shard_map.140 = (f32[256,256]{1,0:T(8,128)S(1)}, f32[4,32,1536]{2,1,0:T(8,128)}, f32[2,32,128]{2,1,0:T(8,128)S(1)}, f32[64,40,128]{2,1,0:T(8,128)}) custom-call(f32[32,6144]{1,0:T(8,128)} %x_ref.1, f32[64,40,128]{2,1,0:T(8,128)S(1)} %get-tuple-element.150.pack_ref, f32[256,6144]{1,0:T(8,128)S(1)} %bitcast.24), custom_call_target="tpu_custom_call" | custom-call | tf_op jit(solution)/shard_map/pallas_call | solution.py:423
  74.6 0.0 copy-done.2
  74.6 0.0 copy-done.4
  74.6 0.0 copy-done.6
  74.7 0.0 copy-done.5
  74.7 0.0 copy-done.7
  74.7 41.5 %conditional.3 = (f32[32,6144]{1,0:T(8,128)}) conditional(s32[]{:T(128)} %convert_element_type.4, (f32[6144]{0:T(1024)S(1)}, f32[32,6144]{1,0:T(8,128)S(1)}, s32[]{:T(128)}, s32[]{:T(128)}, f32[64,40,128]{2,1,0:T(8,128)}, /*index=5*/f32[1,32,128]{2,1,0:T(8,128)S(1)}, f32[2,32,128]{2,1,0:T(8,128)S(1)}, f32[2,32,128]{2,1,0:T(8,128)S(1)}, ...), branch_computations={%region_2.3_spmd.clone, %region_3.4_spmd} | conditional | flops 679479424 | bytes 66863140 | solution.py:510
  74.9 0.1 copy.33
  75.0 0.1 reshape.43
  75.1 0.4 reshape.34
  75.6 0.6 copy.30
  76.2 3.8 %gather_fusion = f32[384,32,96]{2,1,0:T(8,128)} fusion(f32[32,64,96]{2,0,1:T(8,128)S(1)} %copy.30, s32[1024]{0:T(1024)S(1)} %pad_clamp_fusion), kind=kCustom, calls=%fused_computation | custom fusion | bytes 9438720 | tf_op jit(solution)/shard_map/cond/branch_1_fun/gather | solution.py:492
  79.9 17.6 %reshape.35 = f32[64,6,96,96]{3,2,0,1:T(8,128)} reshape(f32[64,6,9216]{2,0,1:T(8,128)} %get-tuple-element.102) | data formatting | bytes 28311552 | tf_op jit(solution)/shard_map/cond/branch_1_fun/reshape | solution.py:493
  97.5 0.0 copy-start.3
  97.5 13.9 %fusion.4 = f32[32,64,96]{2,0,1:T(8,128)S(1)} fusion(f32[32,64,6,96]{3,0,2,1:T(8,128)} %bitcast.27, f32[64,6,96,96]{3,2,0,1:T(8,128)} %reshape.35), kind=kOutput, calls=%fused_computation.7 | convolution fusion | flops 679477248 | bytes 19660800 | tf_op jit(solution)/shard_map/cond/branch_1_fun/kibc,ibrc->kir/dot_general | solution.py:494
  111.4 0.6 copy.32
  112.0 0.6 reshape.36.y_ref
  112.6 0.0 copy-done.3
  112.6 3.5 %branch_1_fun.3 = f32[32,6144]{1,0:T(8,128)} custom-call(f32[32,6144]{1,0:T(8,128)S(1)} %reshape.36.y_ref, f32[4,32,1536]{2,1,0:T(8,128)S(1)} %copy-done.3, s32[4,1536]{1,0:T(4,128)S(1)} %bitcast.29, f32[4,1536]{1,0:T(4,128)S(1)} %bitcast.30), custom_call_target="tpu_custom_call" | custom-call | tf_op jit(solution)/shard_map/cond/branch_1_fun/pallas_call | solution.py:423
  116.2 0.0 copy-start.1
  116.2 2.8 %copy-done.1 = f32[8,32,6144]{2,1,0:T(8,128)S(1)} copy-done((f32[8,32,6144]{2,1,0:T(8,128)S(1)}, f32[8,32,6144]{2,1,0:T(8,128)}, u32[]{:S(2)}) %copy-start.1) | copy-done | bytes 6291480
  119.0 23.7 %shard_map.141 = (f32[32,6144]{1,0:T(8,128)S(1)}, f32[256,32]{1,0:T(8,128)S(1)}, f32[32,32]{1,0:T(8,128)S(1)}) custom-call(f32[32,6144]{1,0:T(8,128)} %get-tuple-element.151.image_ref, f32[256,6144]{1,0:T(8,128)S(1)} %bitcast.25, f32[256,256]{1,0:T(8,128)S(1)} %get-tuple-element.67.cross_ref), custom_call_target="tpu_custom_call" | custom-call | tf_op jit(solution)/shard_map/pallas_call | solution.py:423
  142.7 0.9 copy.46
  143.6 0.7 copy.47
  144.2 0.6 copy.48
  (3 shorter events, 0.0 us)
Async XLA Ops:
  0.6 74.0 %copy-start.2 = (f32[32,6144]{1,0:T(8,128)S(1)}, f32[32,6144]{1,0:T(8,128)}, u32[]{:S(2)}) copy-start(f32[32,6144]{1,0:T(8,128)} %x_ref.1) | copy-start | bytes 2359300
  0.6 74.0 %copy-start.4 = (f32[6144]{0:T(1024)S(1)}, f32[6144]{0:T(1024)}, u32[]{:S(2)}) copy-start(f32[6144]{0:T(1024)} %param.21) | copy-start | bytes 73732
  0.7 74.0 %copy-start.6 = (f32[1,4,1536]{2,1,0:T(4,128)S(1)}, f32[1,4,1536]{2,1,0:T(4,128)}, u32[]{:S(2)}) copy-start(f32[1,4,1536]{2,1,0:T(4,128)} %param.20) | copy-start | bytes 73732
  0.7 74.0 %copy-start.5 = (s32[1,4,1536]{2,1,0:T(4,128)S(1)}, s32[1,4,1536]{2,1,0:T(4,128)}, u32[]{:S(2)}) copy-start(s32[1,4,1536]{2,1,0:T(4,128)} %param.19) | copy-start | bytes 73732
  0.7 74.0 %copy-start.7 = (s32[64,6]{0,1:T(8,128)S(1)}, s32[64,6]{0,1:T(8,128)}, u32[]{:S(2)}) copy-start(s32[64,6]{0,1:T(8,128)} %param.18) | copy-start | bytes 4612
  25.1 2.8 %copy-start = (f32[8,32,6144]{2,1,0:T(8,128)S(1)}, f32[8,32,6144]{2,1,0:T(8,128)}, u32[]{:S(2)}) copy-start(f32[8,32,6144]{2,1,0:T(8,128)} %param.16) | copy-start | bytes 18874372
  97.5 15.1 %copy-start.3 = (f32[4,32,1536]{2,1,0:T(8,128)S(1)}, f32[4,32,1536]{2,1,0:T(8,128)}, u32[]{:S(2)}) copy-start(f32[4,32,1536]{2,1,0:T(8,128)} %get-tuple-element.51.faces_ref) | copy-start | bytes 2359300 | tf_op jit(solution)/shard_map/cond
  116.2 2.8 %copy-start.1 = (f32[8,32,6144]{2,1,0:T(8,128)S(1)}, f32[8,32,6144]{2,1,0:T(8,128)}, u32[]{:S(2)}) copy-start(f32[8,32,6144]{2,1,0:T(8,128)} %param.16) | copy-start | bytes 18874372

commit v3 on v2

--- a/solution.py
+++ b/solution.py
@@ -31,7 +31,31 @@
     return jnp.take_along_axis(x, low, axis=1)
 
 
-def pack_kernel(subdomains, per, x_ref, src_ref, dest_ref, tgt_ref, w_ref, out_ref, meta_ref):
+def wet_kernel(
+    subdomains, per, x_ref, xs_ref, diag_ref, edge_ref, src_ref, dest_ref, tgt_ref, w_ref, out_ref,
+    meta_ref, pack_ref, got_ref, lhs_ref, acc_ref, sems,
+):
+    @pl.when(lax.axis_index("sec") == 1)
+    def _():
+        wet_body(
+            subdomains, per, x_ref, xs_ref, diag_ref, edge_ref, src_ref, dest_ref, tgt_ref, w_ref,
+            out_ref, meta_ref, pack_ref, got_ref, lhs_ref, acc_ref, sems,
+        )
+
+
+def wet_body(
+    subdomains, per, own_ref, x_ref, diag_ref, edge_ref, src_ref, dest_ref, tgt_ref, w_ref, image_ref,
+    meta_ref, pack_ref, got_ref, lhs_ref, acc_ref, sems,
+):
+    mine = lax.axis_index("grp") * lax.axis_size("dev") + lax.axis_index("dev")
+    barrier = pltpu.get_barrier_semaphore()
+
+    def greet(i, carry):
+        other = subdomains + lax.rem(mine + i, subdomains)
+        pl.semaphore_signal(barrier, inc=1, device_id=place(other), device_id_type=MESH)
+        return carry
+
+    lax.fori_loop(1, subdomains, greet, 0)
     width, rows = x_ref.shape
     blocks = src_ref.shape[0]
     slabs = subdomains * per
@@ -79,7 +103,7 @@
     meta_ref[2] = parts[2] * LANES + parts[3]
     meta_ref[3] = parts[4] + parts[5] + parts[6]
 
-    def gather(a, carry):
+    def gather(a, ref, to):
         row = pl.ds(a, 1)
         high = jnp.broadcast_to(meta_ref[0, row, :].astype(jnp.int32), (width, LANES))
         low = jnp.broadcast_to(meta_ref[1, row, :].astype(jnp.int32), (width, LANES))
@@ -87,25 +111,43 @@
         for h in range(rows // LANES):
             piece = lane_gather(x_ref[:, h * LANES : (h + 1) * LANES], low)
             got = jnp.where(high == h, piece, got)
-        out_ref[a, :width, :] = got * meta_ref[3, row, :]
-        out_ref[a, width:, :] = jnp.broadcast_to(meta_ref[2, row, :], (META, LANES))
+        ref[to, :width, :] = got * meta_ref[3, row, :]
+        ref[to, width:, :] = jnp.broadcast_to(meta_ref[2, row, :], (META, LANES))
+
+    def copy(to, at):
+        return remote(
+            pack_ref.at[pl.ds(to * per, per)], got_ref.at[pl.ds(at * per, per)], sems.at[0, to],
+            sems.at[1, at], place(subdomains + to),
+        )
+
+    pl.semaphore_wait(barrier, subdomains - 1)
+
+    def send(s, carry):
+        q = lax.rem(mine + s, subdomains)
+
+        def one(p, inner):
+            gather(q * per + p, pack_ref, q * per + p)
+            return inner
+
+        lax.fori_loop(0, per, one, 0)
+        copy(q, mine).start()
         return carry
 
-    lax.fori_loop(0, slabs, gather, 0)
-
-
-def fluid_kernel(x_ref, diag_ref, left_ref, right_ref, got_ref, out_ref, lhs_ref, acc_ref):
-    width, rows = x_ref.shape
-    slabs = got_ref.shape[0]
+    lax.fori_loop(1, subdomains, send, 0)
+
+    def keep(p, inner):
+        gather(mine * per + p, got_ref, mine * per + p)
+        return inner
+
+    lax.fori_loop(0, per, keep, 0)
     wide = 2 * LANES
     highs = rows // wide
-    group = 4
     acc_ref[...] = jnp.zeros_like(acc_ref)
 
-    def step(g, carry):
+    def add(q):
         ohs = []
-        for s in range(group):
-            a = g * group + s
+        for s in range(per):
+            a = q * per + s
             target = got_ref[a, width : width + 1, :].astype(jnp.int32)
             vals = got_ref[a, :width, :]
             hi = vals.astype(BF16).astype(F32)
@@ -115,26 +157,40 @@
             at = s * wide
             for h in range(highs):
                 hit = high == h
-                lhs_ref[h * width : (h + 1) * width, at : at + LANES] = jnp.where(
-                    hit, hi, 0.0
-                ).astype(BF16)
-                lhs_ref[h * width : (h + 1) * width, at + LANES : at + wide] = jnp.where(
-                    hit, lo, 0.0
-                ).astype(BF16)
+                band = slice(h * width, (h + 1) * width)
+                lhs_ref[band, at : at + LANES] = jnp.where(hit, hi, 0.0).astype(BF16)
+                lhs_ref[band, at + LANES : at + wide] = jnp.where(hit, lo, 0.0).astype(BF16)
             oh = jnp.where(
                 lax.broadcasted_iota(jnp.int32, (wide, LANES), 0) == low, 1.0, 0.0
             ).astype(BF16)
             ohs += [oh, oh]
         acc_ref[...] += nt(lhs_ref[...], jnp.concatenate(ohs, axis=1))
+
+    add(mine)
+
+    def take(s, carry):
+        q = lax.rem(mine + subdomains - s, subdomains)
+        copy(q, q).wait_recv()
+        add(q)
         return carry
 
-    lax.fori_loop(0, slabs // group, step, 0)
+    lax.fori_loop(1, subdomains, take, 0)
+
+    def drain(s, carry):
+        copy(lax.rem(mine + s, subdomains), mine).wait_send()
+        return carry
+
+    lax.fori_loop(1, subdomains, drain, 0)
+    edges = [
+        jnp.where(mine == 0, 0.0, edge_ref[0]),
+        jnp.where(mine == subdomains - 1, 0.0, edge_ref[1]),
+    ]
     lane = lax.broadcasted_iota(jnp.int32, (width, LANES), 1)
     pieces = rows // LANES
     for t in range(pieces):
-        own = x_ref[:, t * LANES : (t + 1) * LANES]
-        prev = left_ref[...] if t == 0 else x_ref[:, (t - 1) * LANES : t * LANES]
-        nxt = right_ref[...] if t == pieces - 1 else x_ref[:, (t + 1) * LANES : (t + 2) * LANES]
+        own = own_ref[:, t * LANES : (t + 1) * LANES]
+        prev = edges[0] if t == 0 else own_ref[:, (t - 1) * LANES : t * LANES]
+        nxt = edges[1] if t == pieces - 1 else own_ref[:, (t + 1) * LANES : (t + 2) * LANES]
         before = jnp.where(lane == 0, pltpu.roll(prev, 1, 1), pltpu.roll(own, 1, 1))
         after = jnp.where(
             lane == LANES - 1, pltpu.roll(nxt, LANES - 1, 1), pltpu.roll(own, LANES - 1, 1)
@@ -142,7 +198,7 @@
         h, side = t // 2, t % 2
         added = acc_ref[h * width : (h + 1) * width, side * LANES : (side + 1) * LANES]
         d = diag_ref[:, t * LANES : (t + 1) * LANES]
-        out_ref[:, t * LANES : (t + 1) * LANES] = d * own - before - after + added
+        image_ref[:, t * LANES : (t + 1) * LANES] = d * own - before - after + added
 
 
 def face_kernel(y_ref, faces_ref, match_ref, weight_ref, out_ref):
@@ -238,8 +294,8 @@
 
 
 def exchange_kernel(
-    subdomains, per, face, x_ref, pack_ref, prior_ref, cross_ref, faces_ref, edge_ref, got_ref,
-    stage, slots, total, sems, face_sems, edge_sems, wet_sems,
+    subdomains, face, x_ref, prior_ref, cross_ref, faces_ref, edge_ref, xs_ref,
+    stage, slots, total, sems, face_sems, edge_sems, twin_sems,
 ):
     n = 2 * subdomains
     me = own_index()
@@ -267,26 +323,16 @@
             edge_sems.at[1, side], place(to),
         )
 
-    def wet_copy(to, at):
-        return remote(
-            pack_ref.at[pl.ds(to * per, per)], got_ref.at[pl.ds(at * per, per)],
-            wet_sems.at[0, to], wet_sems.at[1, at], place(subdomains + to),
-        )
-
-    def each(body):
-        def step(s, carry):
-            body(lax.rem(mine + s, subdomains))
-            return carry
-
-        lax.fori_loop(0, subdomains, step, 0)
+    def twin_copy():
+        return remote(x_ref, xs_ref, twin_sems.at[0], twin_sems.at[1], (1, g, d))
 
     pl.semaphore_wait(announce(me, n), n - 1)
 
     @pl.when(sec == 0)
     def _():
+        twin_copy().start()
         for m in range(ROUNDS):
             face_copy(m).start()
-        each(lambda q: wet_copy(q, mine).start())
 
     @pl.when(sec == 1)
     def _():
@@ -316,13 +362,13 @@
     def _():
         for m in range(ROUNDS):
             face_copy(m).wait()
-        each(lambda q: wet_copy(q, mine).wait_send())
+        twin_copy().wait_send()
 
     @pl.when(sec == 1)
     def _():
         edge_copy(0).wait()
         edge_copy(1).wait()
-        each(lambda q: wet_copy(q, q).wait_recv())
+        twin_copy().wait_recv()
 
 
 def finish_kernel(
@@ -450,29 +496,16 @@
     is_shell = lax.axis_index("sec") == 0
     flat_prior = prior.reshape(-1, local_rows)
     basis = flat_prior.shape[0]
-    tiled = (wet_slots // LANES, LANES)
-
-    def pack(x):
-        return call(
-            functools.partial(pack_kernel, subdomains, per),
-            jax.ShapeDtypeStruct((slabs, width + META, LANES), F32),
-            x, wet_source.reshape(tiled), wet_dest.reshape(tiled), wet_target.reshape(tiled),
-            wet_weight.reshape(tiled), scratch=[pltpu.VMEM((4, slabs, LANES), F32)],
-        )
-
-    packed = lax.cond(
-        is_shell, pack, lambda x: jnp.zeros((slabs, width + META, LANES), F32), current
-    )
     n = 2 * subdomains
-    cross, faces, edges, got = call(
-        functools.partial(exchange_kernel, subdomains, per, face_rows),
+    cross, faces, edges, twin = call(
+        functools.partial(exchange_kernel, subdomains, face_rows),
         (
             jax.ShapeDtypeStruct((basis, basis), F32),
             jax.ShapeDtypeStruct((ROUNDS, width, face_rows), F32),
             jax.ShapeDtypeStruct((2, width, LANES), F32),
-            jax.ShapeDtypeStruct(packed.shape, F32),
+            jax.ShapeDtypeStruct(current.shape, F32),
         ),
-        current, packed, flat_prior,
+        current, flat_prior,
         scratch=[
             pltpu.VMEM((n, basis // n, basis), F32),
             pltpu.VMEM((n, basis // n, basis), F32),
@@ -480,13 +513,28 @@
             pltpu.SemaphoreType.DMA((4, n)),
             pltpu.SemaphoreType.DMA((2, ROUNDS)),
             pltpu.SemaphoreType.DMA((2, 2)),
+            pltpu.SemaphoreType.DMA((2,)),
+        ],
+        ident=0,
+    )
+    tiled = (wet_slots // LANES, LANES)
+    bands = local_rows // (2 * LANES) * width
+    slab = pltpu.VMEM((slabs, width + META, LANES), F32)
+    fluid = call(
+        functools.partial(wet_kernel, subdomains, per),
+        jax.ShapeDtypeStruct((width, local_rows), F32),
+        current, twin, fluid_diag[None, :], edges, wet_source.reshape(tiled),
+        wet_dest.reshape(tiled), wet_target.reshape(tiled), wet_weight.reshape(tiled),
+        scratch=[
+            pltpu.VMEM((4, slabs, LANES), F32),
+            slab,
+            slab,
+            pltpu.VMEM((bands, 2 * per * LANES), BF16),
+            pltpu.VMEM((bands, 2 * LANES), F32),
             pltpu.SemaphoreType.DMA((2, subdomains)),
         ],
-        ident=0,
-    )
-    mine = lax.axis_index("grp") * dev + lax.axis_index("dev")
-    left = jnp.where(mine == 0, 0.0, edges[0])
-    right = jnp.where(mine == subdomains - 1, 0.0, edges[1])
+        ident=2,
+    )
 
     def shell_apply(vector):
         picked = vector.reshape(width, row_blocks, BS)[:, block_cols, :]
@@ -497,17 +545,7 @@
             result.reshape(width, local_rows), faces, face_match[0], face_weight[0],
         )
 
-    def fluid_apply(vector):
-        return call(
-            fluid_kernel, jax.ShapeDtypeStruct((width, local_rows), F32),
-            vector, fluid_diag[None, :], left, right, got,
-            scratch=[
-                pltpu.VMEM((local_rows // 256 * width, 8 * LANES), BF16),
-                pltpu.VMEM((local_rows // 256 * width, 2 * LANES), F32),
-            ],
-        )
-
-    image = lax.cond(is_shell, shell_apply, fluid_apply, current)
+    image = lax.cond(is_shell, shell_apply, lambda x: fluid, current)
     lanes = -(-(basis + width) // LANES) * LANES
     cuts = n // width
     piece = pltpu.VMEM((n, 1, lanes // cuts), F32)

time: 146 us -> 112 us (0.77)
  Pallas kernels: 98.3 us -> 61.5 us
  local copies, waits for them, and re-layouts: 31.6 us -> 35.1 us
    pallas_call x4, Pallas kernels: 98.3 us -> 61.5 us  [call(): pl.pallas_call(kernel, out_shape=out_shape, in_specs=[spec] * len(args),...]
    unnamed x17 -> x25, local copies, waits for them, and re-layouts: 7.73 us -> 11.3 us
where the time goes in v3:
time: 112 us; the launch traced here: 111 us
  Pallas kernels  61.5 us (55%)
  local copies, waits for them, and re-layouts  35.1 us (31%)
  matrix products  13.8 us (12%)
    pallas_call x4, Pallas kernels, call(): pl.pallas_call(kernel, out_shape=out_shape, in_specs=[spec] * len(args),...  61.5 us
    reshape x1, local copies, waits for them, and re-layouts, shell_apply(): matrices = block_values.reshape(row_blocks, NB, BS, BS)  17.6 us
    dot_general x1, matrix products, shell_apply(): result = jnp.einsum('kibc,ibrc->kir', picked, matrices, precision=high)  13.8 us
    unnamed x25, local copies, waits for them, and re-layouts  11.3 us
    gather x1, local copies, waits for them, and re-layouts, shell_apply(): picked = vector.reshape(width, row_blocks, BS)[:, block_cols, :]  3.76 us

profile of v3, /device:TPU:0, one launch (start us, length us, event | category | flops | bytes accessed | tf_op | source)
XLA Modules:
  0.0 111.4 jit_solution(9179437304851166902)
XLA Ops:
  0.6 0.0 copy-start.10
  0.6 0.0 copy-start
  0.7 2.8 %copy-done = f32[8,32,6144]{2,1,0:T(8,128)S(1)} copy-done((f32[8,32,6144]{2,1,0:T(8,128)S(1)}, f32[8,32,6144]{2,1,0:T(8,128)}, u32[]{:S(2)}) %copy-start) | copy-done | bytes 6291480
  3.4 0.0 copy-start.7
  3.4 0.0 copy-start.8
  3.4 0.0 copy-start.9
  3.4 31.5 %shard_map.134 = (f32[256,256]{1,0:T(8,128)S(1)}, f32[4,32,1536]{2,1,0:T(8,128)S(1)}, f32[2,32,128]{2,1,0:T(8,128)S(1)}, f32[32,6144]{1,0:T(8,128)S(1)}) custom-call(f32[32,6144]{1,0:T(8,128)} %x_ref.3, f32[256,6144]{1,0:T(8,128)S(1)} %bitcast.20), custom_call_target="tpu_custom_call" | custom-call | tf_op jit(solution)/shard_map/pallas_call | solution.py:469
  35.0 0.0 copy-start.2
  35.0 0.7 copy-done.2
  35.7 0.0 copy-start.3
  35.7 0.7 copy-done.3
  36.4 0.0 copy-start.4
  36.4 0.7 copy-done.4
  37.1 0.0 copy-start.5
  37.1 0.7 copy-done.5
  37.8 0.0 copy-start.6
  37.8 0.7 copy-done.6
  38.5 2.4 %shard_map.135 = f32[32,6144]{1,0:T(8,128)} custom-call(f32[32,6144]{1,0:T(8,128)} %x_ref.3, f32[32,6144]{1,0:T(8,128)S(1)} %get-tuple-element.32.xs_ref, f32[1,6144]{1,0:T(1,128)S(1)} %bitcast.23, f32[2,32,128]{2,1,0:T(8,128)S(1)} %get-tuple-element.33.edge_ref, s32[24,128]{1,0:T(8,128)S(1)} %bitcast.24, s32[24,128]{1,0:T(8,128)S(1)} %bitcast.25, ...), custom_call_target="tpu_custom_call" | custom-call | tf_op jit(solution)/shard_map/pallas_call | solution.py:469
  40.9 0.0 copy-done.10
  40.9 0.0 copy-done.7
  41.0 0.0 copy-done.8
  41.0 0.0 copy-done.9
  41.0 41.5 %conditional.1 = (f32[32,6144]{1,0:T(8,128)}) conditional(s32[]{:T(128)} %convert_element_type.3, f32[32,6144]{1,0:T(8,128)} %shard_map.135, (f32[32,6144]{1,0:T(8,128)S(1)}, s32[64,6]{0,1:T(8,128)S(1)}, f32[64,6,9216]{2,0,1:T(8,128)}, s32[1,4,1536]{2,1,0:T(4,128)S(1)}, f32[1,4,1536]{2,1,0:T(4,128)S(1)}, /*index=5*/f32[4,32,1536]{2,1,0:T(8,128)S(1)}) %tuple.26), branch_computations={%region_0.0_spmd, %region_1.0_spmd} | conditional | flops 679479424 | bytes 63717384 | solution.py:548
  41.2 0.1 copy.27
  41.3 0.1 reshape.41
  41.4 0.4 reshape.24
  41.8 0.6 copy.24
  42.5 3.8 %gather_fusion = f32[384,32,96]{2,1,0:T(8,128)} fusion(f32[32,64,96]{2,0,1:T(8,128)S(1)} %copy.24, s32[1024]{0:T(1024)S(1)} %pad_clamp_fusion), kind=kCustom, calls=%fused_computation | custom fusion | bytes 9438720 | tf_op jit(solution)/shard_map/cond/branch_1_fun/gather | solution.py:540
  46.2 17.6 %reshape.25 = f32[64,6,96,96]{3,2,0,1:T(8,128)} reshape(f32[64,6,9216]{2,0,1:T(8,128)} %get-tuple-element.44) | data formatting | bytes 28311552 | tf_op jit(solution)/shard_map/cond/branch_1_fun/reshape | solution.py:541
  63.8 13.8 %fusion.2 = f32[32,64,96]{2,0,1:T(8,128)S(1)} fusion(f32[32,64,6,96]{3,0,2,1:T(8,128)} %bitcast.28, f32[64,6,96,96]{3,2,0,1:T(8,128)} %reshape.25), kind=kOutput, calls=%fused_computation.3 | convolution fusion | flops 679477248 | bytes 19660800 | tf_op jit(solution)/shard_map/cond/branch_1_fun/kibc,ibrc->kir/dot_general | solution.py:542
  77.6 0.6 copy.26
  78.3 0.6 reshape.26.y_ref
  78.9 3.6 %branch_1_fun.1 = f32[32,6144]{1,0:T(8,128)} custom-call(f32[32,6144]{1,0:T(8,128)S(1)} %reshape.26.y_ref, f32[4,32,1536]{2,1,0:T(8,128)S(1)} %get-tuple-element.19.faces_ref, s32[4,1536]{1,0:T(4,128)S(1)} %bitcast.29, f32[4,1536]{1,0:T(4,128)S(1)} %bitcast.30), custom_call_target="tpu_custom_call" | custom-call | tf_op jit(solution)/shard_map/cond/branch_1_fun/pallas_call | solution.py:469
  82.5 0.0 copy-start.1
  82.5 2.8 %copy-done.1 = f32[8,32,6144]{2,1,0:T(8,128)S(1)} copy-done((f32[8,32,6144]{2,1,0:T(8,128)S(1)}, f32[8,32,6144]{2,1,0:T(8,128)}, u32[]{:S(2)}) %copy-start.1) | copy-done | bytes 6291480
  85.3 23.9 %shard_map.136 = (f32[32,6144]{1,0:T(8,128)S(1)}, f32[256,32]{1,0:T(8,128)S(1)}, f32[32,32]{1,0:T(8,128)S(1)}) custom-call(f32[32,6144]{1,0:T(8,128)} %get-tuple-element.71.image_ref, f32[256,6144]{1,0:T(8,128)S(1)} %bitcast.21, f32[256,256]{1,0:T(8,128)S(1)} %get-tuple-element.35.cross_ref), custom_call_target="tpu_custom_call" | custom-call | tf_op jit(solution)/shard_map/pallas_call | solution.py:469
  109.2 0.9 copy.38
  110.1 0.7 copy.39
  110.8 0.6 copy.40
  (2 shorter events, 0.0 us)
Async XLA Ops:
  0.6 40.3 %copy-start.10 = (s32[64,6]{0,1:T(8,128)S(1)}, s32[64,6]{0,1:T(8,128)}, u32[]{:S(2)}) copy-start(s32[64,6]{0,1:T(8,128)} %param.16) | copy-start | bytes 4612
  0.6 2.8 %copy-start = (f32[8,32,6144]{2,1,0:T(8,128)S(1)}, f32[8,32,6144]{2,1,0:T(8,128)}, u32[]{:S(2)}) copy-start(f32[8,32,6144]{2,1,0:T(8,128)} %param.14) | copy-start | bytes 18874372
  3.4 37.5 %copy-start.7 = (f32[32,6144]{1,0:T(8,128)S(1)}, f32[32,6144]{1,0:T(8,128)}, u32[]{:S(2)}) copy-start(f32[32,6144]{1,0:T(8,128)} %x_ref.3) | copy-start | bytes 2359300
  3.4 37.5 %copy-start.8 = (s32[1,4,1536]{2,1,0:T(4,128)S(1)}, s32[1,4,1536]{2,1,0:T(4,128)}, u32[]{:S(2)}) copy-start(s32[1,4,1536]{2,1,0:T(4,128)} %param.17) | copy-start | bytes 73732
  3.4 37.5 %copy-start.9 = (f32[1,4,1536]{2,1,0:T(4,128)S(1)}, f32[1,4,1536]{2,1,0:T(4,128)}, u32[]{:S(2)}) copy-start(f32[1,4,1536]{2,1,0:T(4,128)} %param.18) | copy-start | bytes 73732
  35.0 0.7 copy-start.2
  35.7 0.7 copy-start.3
  36.4 0.7 copy-start.4
  37.1 0.7 copy-start.5
  37.8 0.7 copy-start.6
  82.5 2.8 %copy-start.1 = (f32[8,32,6144]{2,1,0:T(8,128)S(1)}, f32[8,32,6144]{2,1,0:T(8,128)}, u32[]{:S(2)}) copy-start(f32[8,32,6144]{2,1,0:T(8,128)} %param.14) | copy-start | bytes 18874372

commit v4 on v3

--- a/solution.py
+++ b/solution.py
@@ -236,21 +236,40 @@
     return (lax.axis_index("sec") * grp + lax.axis_index("grp")) * dev + lax.axis_index("dev")
 
 
-def everyone(me, n, body):
-    def step(s, carry):
-        body(lax.rem(me + s, n))
-        return carry
-
-    lax.fori_loop(1, n, step, 0)
-
-
-def announce(me, n):
+def everyone(body):
+    counts = [lax.axis_size(axis) for axis in ALL]
+    turns = []
+    for axis, count in zip(ALL, counts):
+        at = lax.axis_index(axis)
+        ring = [at]
+        for _ in range(1, count):
+            following = ring[-1] + 1
+            ring.append(jnp.where(following == count, 0, following))
+        turns.append(ring)
+    for i in range(counts[0]):
+        for j in range(counts[1]):
+            for k in range(counts[2]):
+                if i or j or k:
+                    where = (turns[0][i], turns[1][j], turns[2][k])
+                    body((where[0] * counts[1] + where[1]) * counts[2] + where[2], where)
+
+
+def announce():
     barrier = pltpu.get_barrier_semaphore()
     everyone(
-        me, n,
-        lambda d: pl.semaphore_signal(barrier, inc=1, device_id=place(d), device_id_type=MESH),
+        lambda d, where: pl.semaphore_signal(
+            barrier, inc=1, device_id=where, device_id_type=MESH
+        )
     )
     return barrier
+
+
+def stream(prior_ref, held, sems, chunk):
+    def copy(i):
+        at = pl.ds(pl.multiple_of(i * chunk, chunk), chunk)
+        return pltpu.make_async_copy(prior_ref.at[:, at], held.at[:, at], sems.at[i])
+
+    return copy
 
 
 def remote(src, dst, send, recv, device):
@@ -265,37 +284,40 @@
         self.me, self.n = me, n
         self.stage, self.slots, self.total, self.sems = stage, slots, total, sems
 
-    def piece(self, to, at):
+    def scatter(self):
+        everyone(
+            lambda d, where: remote(
+                self.stage.at[d], self.slots.at[self.me], self.sems.at[0], self.sems.at[1], where
+            ).start()
+        )
+
+    def bulk(self, source, target, first):
+        rest = pl.ds(0, self.n - 1)
+        other = (1 - lax.axis_index("sec"), lax.axis_index("grp"), lax.axis_index("dev"))
         return remote(
-            self.stage.at[to], self.slots.at[at], self.sems.at[0, to], self.sems.at[1, at],
-            place(to),
-        )
-
-    def whole(self, to, at):
-        return remote(
-            self.total.at[at], self.total.at[at], self.sems.at[2, to], self.sems.at[3, at],
-            place(to),
-        )
-
-    def scatter(self):
-        everyone(self.me, self.n, lambda d: self.piece(d, self.me).start())
+            source.at[rest], target.at[rest], self.sems.at[first], self.sems.at[first + 1], other
+        )
 
     def gather(self):
         me = self.me
-        everyone(me, self.n, lambda d: self.piece(d, d).wait_recv())
+        self.bulk(self.stage, self.slots, 0).wait_recv()
         self.slots[me] = self.stage[me]
         self.total[me] = jnp.sum(self.slots[...], axis=0)
-        everyone(me, self.n, lambda d: self.whole(d, me).start())
+        everyone(
+            lambda d, where: remote(
+                self.total.at[me], self.total.at[me], self.sems.at[2], self.sems.at[3], where
+            ).start()
+        )
 
     def finish(self):
-        everyone(self.me, self.n, lambda d: self.whole(d, d).wait_recv())
-        everyone(self.me, self.n, lambda d: self.piece(d, d).wait_send())
-        everyone(self.me, self.n, lambda d: self.whole(d, self.me).wait_send())
+        self.bulk(self.total, self.total, 2).wait_recv()
+        self.bulk(self.stage, self.slots, 0).wait_send()
+        self.bulk(self.total, self.total, 2).wait_send()
 
 
 def exchange_kernel(
     subdomains, face, x_ref, prior_ref, cross_ref, faces_ref, edge_ref, xs_ref,
-    stage, slots, total, sems, face_sems, edge_sems, twin_sems,
+    stage, slots, total, sems, face_sems, edge_sems, twin_sems, held, held_sems,
 ):
     n = 2 * subdomains
     me = own_index()
@@ -326,7 +348,11 @@
     def twin_copy():
         return remote(x_ref, xs_ref, twin_sems.at[0], twin_sems.at[1], (1, g, d))
 
-    pl.semaphore_wait(announce(me, n), n - 1)
+    chunk = held.shape[1] // held_sems.shape[0]
+    incoming = stream(prior_ref, held, held_sems, chunk)
+    for i in range(rows // chunk):
+        incoming(i).start()
+    pl.semaphore_wait(announce(), n - 1)
 
     @pl.when(sec == 0)
     def _():
@@ -340,11 +366,11 @@
         edge_copy(1).start()
 
     basis = prior_ref.shape[0]
-    chunk = 1024
 
     def product(i, carry):
         same, mixed = carry
-        hi, lo = split2(prior_ref[:, pl.ds(pl.multiple_of(i * chunk, chunk), chunk)])
+        incoming(i).wait()
+        hi, lo = split2(held[:, pl.ds(pl.multiple_of(i * chunk, chunk), chunk)])
         return same + nt(hi, hi), mixed + nt(hi, lo)
 
     zero = jnp.zeros((basis, basis), F32)
@@ -373,19 +399,23 @@
 
 def finish_kernel(
     subdomains, total_rows, image_ref, prior_ref, cross_ref, next_ref, coef_ref, fac_ref,
-    high_ref, low_ref, stage, slots, total, sems,
+    high_ref, low_ref, stage, slots, total, sems, held, held_sems,
 ):
     n = 2 * subdomains
     me = own_index()
     width, rows = image_ref.shape
     basis = prior_ref.shape[0]
-    chunk = 1024
-    barrier = announce(me, n)
+    chunk = held.shape[1] // held_sems.shape[0]
+    incoming = stream(prior_ref, held, held_sems, chunk)
+    for i in range(rows // chunk):
+        incoming(i).start()
+    barrier = announce()
 
     def product(i, carry):
         head, square = carry
         at = pl.ds(pl.multiple_of(i * chunk, chunk), chunk)
-        hi, lo = split2(prior_ref[:, at])
+        incoming(i).wait()
+        hi, lo = split2(held[:, at])
         high_ref[:, at] = hi
         low_ref[:, at] = lo
         ih, il = split2(image_ref[:, at])
@@ -463,13 +493,15 @@
     lax.fori_loop(0, rows // chunk, out, 0)
 
 
-def call(kernel, out_shape, *args, scratch=(), ident=None):
+def call(kernel, out_shape, *args, scratch=(), ident=None, kept=()):
     multi = isinstance(out_shape, (list, tuple))
     spec = pl.BlockSpec(memory_space=pltpu.VMEM)
     return pl.pallas_call(
         kernel,
         out_shape=out_shape,
-        in_specs=[spec] * len(args),
+        in_specs=[
+            pl.BlockSpec(memory_space=pltpu.HBM) if i in kept else spec for i in range(len(args))
+        ],
         out_specs=tuple([spec] * len(out_shape)) if multi else spec,
         scratch_shapes=list(scratch),
         compiler_params=pltpu.CompilerParams(
@@ -497,6 +529,10 @@
     flat_prior = prior.reshape(-1, local_rows)
     basis = flat_prior.shape[0]
     n = 2 * subdomains
+    stream_scratch = [
+        pltpu.VMEM((basis, local_rows), F32),
+        pltpu.SemaphoreType.DMA((local_rows // 1024,)),
+    ]
     cross, faces, edges, twin = call(
         functools.partial(exchange_kernel, subdomains, face_rows),
         (
@@ -510,12 +546,13 @@
             pltpu.VMEM((n, basis // n, basis), F32),
             pltpu.VMEM((n, basis // n, basis), F32),
             pltpu.VMEM((n, basis // n, basis), F32),
-            pltpu.SemaphoreType.DMA((4, n)),
+            pltpu.SemaphoreType.DMA((4,)),
             pltpu.SemaphoreType.DMA((2, ROUNDS)),
             pltpu.SemaphoreType.DMA((2, 2)),
             pltpu.SemaphoreType.DMA((2,)),
+            *stream_scratch,
         ],
-        ident=0,
+        ident=0, kept=(1,),
     )
     tiled = (wet_slots // LANES, LANES)
     bands = local_rows // (2 * LANES) * width
@@ -561,9 +598,10 @@
             pltpu.VMEM((basis, local_rows), BF16),
             pltpu.VMEM((basis, local_rows), BF16),
             piece, piece, piece,
-            pltpu.SemaphoreType.DMA((4, n)),
+            pltpu.SemaphoreType.DMA((4,)),
+            *stream_scratch,
         ],
-        ident=1,
+        ident=1, kept=(1,),
     )
     return (next_block, coef.reshape(prior.shape[0], width, width), factor)
 

time: 112 us -> 107 us (0.955)
  Pallas kernels: 61.5 us -> 56.3 us
    pallas_call x4, Pallas kernels: 61.5 us -> 56.3 us  [call(): pl.pallas_call(kernel, out_shape=out_shape, in_specs=[pl.BlockSpec(memory...]
where the time goes in v4:
time: 107 us; the launch traced here: 106 us
  Pallas kernels  56.3 us (53%)
  local copies, waits for them, and re-layouts  35.1 us (33%)
  matrix products  13.8 us (13%)
    pallas_call x4, Pallas kernels, call(): pl.pallas_call(kernel, out_shape=out_shape, in_specs=[pl.BlockSpec(memory...  56.3 us
    reshape x1, local copies, waits for them, and re-layouts, shell_apply(): matrices = block_values.reshape(row_blocks, NB, BS, BS)  17.6 us
    dot_general x1, matrix products, shell_apply(): result = jnp.einsum('kibc,ibrc->kir', picked, matrices, precision=high)  13.8 us
    unnamed x25, local copies, waits for them, and re-layouts  11.3 us
    gather x1, local copies, waits for them, and re-layouts, shell_apply(): picked = vector.reshape(width, row_blocks, BS)[:, block_cols, :]  3.76 us

profile of v4, /device:TPU:0, one launch (start us, length us, event | category | flops | bytes accessed | tf_op | source)
XLA Modules:
  0.0 106.2 jit_solution(2080030771860973559)
XLA Ops:
  0.6 0.0 copy-start.10
  0.6 0.0 copy-start
  0.7 2.8 %copy-done = f32[8,32,6144]{2,1,0:T(8,128)S(1)} copy-done((f32[8,32,6144]{2,1,0:T(8,128)S(1)}, f32[8,32,6144]{2,1,0:T(8,128)}, u32[]{:S(2)}) %copy-start) | copy-done | bytes 6291480
  3.4 0.0 copy-start.7
  3.4 0.0 copy-start.8
  3.4 0.0 copy-start.9
  3.4 29.2 %shard_map.134 = (f32[256,256]{1,0:T(8,128)S(1)}, f32[4,32,1536]{2,1,0:T(8,128)S(1)}, f32[2,32,128]{2,1,0:T(8,128)S(1)}, f32[32,6144]{1,0:T(8,128)S(1)}) custom-call(f32[32,6144]{1,0:T(8,128)} %x_ref.3, f32[256,6144]{1,0:T(8,128)S(1)} %bitcast.20), custom_call_target="tpu_custom_call" | custom-call | tf_op jit(solution)/shard_map/pallas_call | solution.py:499
  32.7 0.0 copy-start.2
  32.7 0.7 copy-done.2
  33.4 0.0 copy-start.3
  33.4 0.7 copy-done.3
  34.1 0.0 copy-start.4
  34.1 0.7 copy-done.4
  34.9 0.0 copy-start.5
  34.9 0.7 copy-done.5
  35.6 0.0 copy-start.6
  35.6 0.7 copy-done.6
  36.3 2.4 %shard_map.135 = f32[32,6144]{1,0:T(8,128)} custom-call(f32[32,6144]{1,0:T(8,128)} %x_ref.3, f32[32,6144]{1,0:T(8,128)S(1)} %get-tuple-element.32.xs_ref, f32[1,6144]{1,0:T(1,128)S(1)} %bitcast.23, f32[2,32,128]{2,1,0:T(8,128)S(1)} %get-tuple-element.33.edge_ref, s32[24,128]{1,0:T(8,128)S(1)} %bitcast.24, s32[24,128]{1,0:T(8,128)S(1)} %bitcast.25, ...), custom_call_target="tpu_custom_call" | custom-call | tf_op jit(solution)/shard_map/pallas_call | solution.py:499
  38.7 0.0 copy-done.10
  38.7 0.0 copy-done.7
  38.7 0.0 copy-done.8
  38.7 0.0 copy-done.9
  38.7 41.5 %conditional.1 = (f32[32,6144]{1,0:T(8,128)}) conditional(s32[]{:T(128)} %convert_element_type.3, f32[32,6144]{1,0:T(8,128)} %shard_map.135, (f32[32,6144]{1,0:T(8,128)S(1)}, s32[64,6]{0,1:T(8,128)S(1)}, f32[64,6,9216]{2,0,1:T(8,128)}, s32[1,4,1536]{2,1,0:T(4,128)S(1)}, f32[1,4,1536]{2,1,0:T(4,128)S(1)}, /*index=5*/f32[4,32,1536]{2,1,0:T(8,128)S(1)}) %tuple.26), branch_computations={%region_0.0_spmd, %region_1.0_spmd} | conditional | flops 679479424 | bytes 63717384 | solution.py:585
  38.9 0.1 copy.27
  39.0 0.1 reshape.41
  39.2 0.4 reshape.24
  39.6 0.6 copy.24
  40.2 3.8 %gather_fusion = f32[384,32,96]{2,1,0:T(8,128)} fusion(f32[32,64,96]{2,0,1:T(8,128)S(1)} %copy.24, s32[1024]{0:T(1024)S(1)} %pad_clamp_fusion), kind=kCustom, calls=%fused_computation | custom fusion | bytes 9438720 | tf_op jit(solution)/shard_map/cond/branch_1_fun/gather | solution.py:577
  44.0 17.6 %reshape.25 = f32[64,6,96,96]{3,2,0,1:T(8,128)} reshape(f32[64,6,9216]{2,0,1:T(8,128)} %get-tuple-element.44) | data formatting | bytes 28311552 | tf_op jit(solution)/shard_map/cond/branch_1_fun/reshape | solution.py:578
  61.6 13.8 %fusion.2 = f32[32,64,96]{2,0,1:T(8,128)S(1)} fusion(f32[32,64,6,96]{3,0,2,1:T(8,128)} %bitcast.28, f32[64,6,96,96]{3,2,0,1:T(8,128)} %reshape.25), kind=kOutput, calls=%fused_computation.3 | convolution fusion | flops 679477248 | bytes 19660800 | tf_op jit(solution)/shard_map/cond/branch_1_fun/kibc,ibrc->kir/dot_general | solution.py:579
  75.4 0.6 copy.26
  76.0 0.6 reshape.26.y_ref
  76.6 3.6 %branch_1_fun.1 = f32[32,6144]{1,0:T(8,128)} custom-call(f32[32,6144]{1,0:T(8,128)S(1)} %reshape.26.y_ref, f32[4,32,1536]{2,1,0:T(8,128)S(1)} %get-tuple-element.19.faces_ref, s32[4,1536]{1,0:T(4,128)S(1)} %bitcast.29, f32[4,1536]{1,0:T(4,128)S(1)} %bitcast.30), custom_call_target="tpu_custom_call" | custom-call | tf_op jit(solution)/shard_map/cond/branch_1_fun/pallas_call | solution.py:499
  80.3 0.0 copy-start.1
  80.3 2.8 %copy-done.1 = f32[8,32,6144]{2,1,0:T(8,128)S(1)} copy-done((f32[8,32,6144]{2,1,0:T(8,128)S(1)}, f32[8,32,6144]{2,1,0:T(8,128)}, u32[]{:S(2)}) %copy-start.1) | copy-done | bytes 6291480
  83.0 21.0 %shard_map.136 = (f32[32,6144]{1,0:T(8,128)S(1)}, f32[256,32]{1,0:T(8,128)S(1)}, f32[32,32]{1,0:T(8,128)S(1)}) custom-call(f32[32,6144]{1,0:T(8,128)} %get-tuple-element.71.image_ref, f32[256,6144]{1,0:T(8,128)S(1)} %bitcast.21, f32[256,256]{1,0:T(8,128)S(1)} %get-tuple-element.35.cross_ref), custom_call_target="tpu_custom_call" | custom-call | tf_op jit(solution)/shard_map/pallas_call | solution.py:499
  104.0 0.9 copy.38
  104.9 0.7 copy.39
  105.6 0.6 copy.40
  (2 shorter events, 0.0 us)
Async XLA Ops:
  0.6 38.0 %copy-start.10 = (s32[64,6]{0,1:T(8,128)S(1)}, s32[64,6]{0,1:T(8,128)}, u32[]{:S(2)}) copy-start(s32[64,6]{0,1:T(8,128)} %param.16) | copy-start | bytes 4612
  0.6 2.8 %copy-start = (f32[8,32,6144]{2,1,0:T(8,128)S(1)}, f32[8,32,6144]{2,1,0:T(8,128)}, u32[]{:S(2)}) copy-start(f32[8,32,6144]{2,1,0:T(8,128)} %param.14) | copy-start | bytes 18874372
  3.4 35.2 %copy-start.7 = (f32[32,6144]{1,0:T(8,128)S(1)}, f32[32,6144]{1,0:T(8,128)}, u32[]{:S(2)}) copy-start(f32[32,6144]{1,0:T(8,128)} %x_ref.3) | copy-start | bytes 2359300
  3.4 35.3 %copy-start.8 = (s32[1,4,1536]{2,1,0:T(4,128)S(1)}, s32[1,4,1536]{2,1,0:T(4,128)}, u32[]{:S(2)}) copy-start(s32[1,4,1536]{2,1,0:T(4,128)} %param.17) | copy-start | bytes 73732
  3.4 35.3 %copy-start.9 = (f32[1,4,1536]{2,1,0:T(4,128)S(1)}, f32[1,4,1536]{2,1,0:T(4,128)}, u32[]{:S(2)}) copy-start(f32[1,4,1536]{2,1,0:T(4,128)} %param.18) | copy-start | bytes 73732
  32.7 0.7 copy-start.2
  33.4 0.7 copy-start.3
  34.1 0.7 copy-start.4
  34.9 0.7 copy-start.5
  35.6 0.7 copy-start.6
  80.3 2.8 %copy-start.1 = (f32[8,32,6144]{2,1,0:T(8,128)S(1)}, f32[8,32,6144]{2,1,0:T(8,128)}, u32[]{:S(2)}) copy-start(f32[8,32,6144]{2,1,0:T(8,128)} %param.14) | copy-start | bytes 18874372
